TPU v7x, 32 devices: a whole 2x2x4 slice. The times are simulated.
32 devices in a mesh: req: 16 (over z, y, x), mlp: 2 (over core).
Axes of the slice: x: 2, y: 2, z: 4, core: 2. Of those that a mesh axis runs over, the one named last changes fastest.
Arguments:
- queries: bfloat16 [16, 256, 1536], P('req'), may hold values from -90 to 90
- cached_key_slots: bfloat16 [16, 8192, 512], P('req', 'mlp'), may hold values from -5 to 5
- cached_value_slots: bfloat16 [16, 8192, 512], P('req', 'mlp'), may hold values from -6 to 6
- new_token_keys: bfloat16 [16, 256, 512], P('req', 'mlp'), may hold values from -5.05 to 5.05
- new_token_values: bfloat16 [16, 256, 512], P('req', 'mlp'), may hold values from -6 to 6
- cache_len: int32 [16], replicated, may hold values from 1 to 8192, 65536 in all
- placing: int32 [16], replicated, may hold values from 0 to 15, each once
- w_gate: bfloat16 [1536, 12288], P('req', 'mlp'), may hold values from -0.15625 to 0.15625
- w_up: bfloat16 [1536, 12288], P('req', 'mlp'), may hold values from -0.15625 to 0.15625
- w_down: bfloat16 [12288, 1536], P('mlp', 'req'), may hold values from -0.0546875 to 0.0546875
Outputs:
- mixed: bfloat16 [16, 256, 1536], P('req', 'mlp')
All inputs are finite; a program needn't handle non-finite values.
Results may differ from a plain program's by a relative error of at most 0.019.
Values may be sent and summed in bfloat16 or wider, within the bound.
A program may use at most 192 MiB of HBM per device.

v0:
```python
import jax
import jax.numpy as jnp
from jax import lax
from jax.sharding import PartitionSpec as P

HEAD_SIZE = 256
QUERY_HEADS = 6
KEY_VALUE_HEADS = 2


score_scale = 0.0625
negative = -1e30


def lookup(table, index):
    positions = jnp.arange(table.shape[0], dtype=jnp.int32)
    return jnp.sum(jnp.where(positions == index, table, 0))


def rms_rows(attended):
    wide = attended.astype(jnp.float32)
    return (wide * lax.rsqrt(jnp.mean(wide * wide, axis=-1, keepdims=True) + 1e-06)).astype(
        jnp.bfloat16
    )


def body(
    queries,
    cached_key_slots,
    cached_value_slots,
    new_token_keys,
    new_token_values,
    cache_len,
    placing,
    w_gate,
    w_up,
    w_down,
):
    slot_index = lax.axis_index("req")
    mlp_index = lax.axis_index("mlp")
    mlp_count = lax.axis_size("mlp")
    token_inputs = queries.shape[1]
    request_cache = cached_key_slots.shape[1]
    request_new_tokens = new_token_keys.shape[1]
    query_group_width = QUERY_HEADS // KEY_VALUE_HEADS
    row_count = token_inputs // mlp_count
    request = lookup(placing, slot_index)
    live_len = lookup(cache_len, request)
    query_head_rows = queries[0].reshape(
        token_inputs, KEY_VALUE_HEADS, query_group_width, HEAD_SIZE
    )
    request_keys = cached_key_slots[0].reshape(request_cache, KEY_VALUE_HEADS, HEAD_SIZE)
    request_values = cached_value_slots[0].reshape(request_cache, KEY_VALUE_HEADS, HEAD_SIZE)
    new_key_rows = new_token_keys[0].reshape(request_new_tokens, KEY_VALUE_HEADS, HEAD_SIZE)
    new_value_rows = new_token_values[0].reshape(request_new_tokens, KEY_VALUE_HEADS, HEAD_SIZE)
    cache_pos = mlp_index * request_cache + jnp.arange(request_cache, dtype=jnp.int32)
    cache_live = cache_pos < live_len
    scores_old = (
        jnp.einsum(
            "ngrd,cgd->grnc", query_head_rows, request_keys, preferred_element_type=jnp.float32
        )
        * score_scale
    )
    scores_old = jnp.where(cache_live[None, None, None, :], scores_old, negative)
    fresh_pos = mlp_index * request_new_tokens + jnp.arange(request_new_tokens, dtype=jnp.int32)
    causal = fresh_pos[None, :] <= jnp.arange(token_inputs, dtype=jnp.int32)[:, None]
    scores_new = (
        jnp.einsum(
            "ngrd,mgd->grnm", query_head_rows, new_key_rows, preferred_element_type=jnp.float32
        )
        * score_scale
    )
    scores_new = jnp.where(causal[None, None], scores_new, negative)
    local_top = jnp.maximum(scores_old.max(-1), scores_new.max(-1))
    row_top = lax.pmax(local_top, "mlp")
    expo_old = jnp.exp(scores_old - row_top[..., None])
    expo_new = jnp.exp(scores_new - row_top[..., None])
    denom_local = expo_old.sum(-1) + expo_new.sum(-1)
    probs_old = expo_old.astype(jnp.bfloat16)
    probs_new = expo_new.astype(jnp.bfloat16)
    weighted = jnp.einsum(
        "grnc,cgd->ngrd", probs_old, request_values, preferred_element_type=jnp.float32
    )
    weighted = weighted + jnp.einsum(
        "grnm,mgd->ngrd", probs_new, new_value_rows, preferred_element_type=jnp.float32
    )
    weighted, denom = lax.psum((weighted, denom_local), "mlp")
    attended = (
        (weighted / jnp.transpose(denom, (2, 0, 1))[..., None])
        .reshape(token_inputs, QUERY_HEADS * HEAD_SIZE)
        .astype(jnp.bfloat16)
    )
    normed = rms_rows(attended)
    own_attended = lax.dynamic_slice_in_dim(attended, mlp_index * row_count, row_count, 0)
    gate_sum = jnp.dot(
        normed,
        lax.all_gather(w_gate, "req", axis=0, tiled=True),
        preferred_element_type=jnp.float32,
    )
    upper_sum = jnp.dot(
        normed, lax.all_gather(w_up, "req", axis=0, tiled=True), preferred_element_type=jnp.float32
    )
    hidden = (jax.nn.silu(gate_sum) * upper_sum).astype(jnp.bfloat16)
    partial_down = jnp.dot(
        hidden,
        lax.all_gather(w_down, "req", axis=1, tiled=True),
        preferred_element_type=jnp.float32,
    )
    own_rows = lax.psum_scatter(
        partial_down.astype(jnp.bfloat16), "mlp", scatter_dimension=0, tiled=True
    ).astype(jnp.float32)
    residual = own_attended.astype(jnp.float32)
    return (residual + own_rows).astype(jnp.bfloat16)[None]


def solution(mesh):
    in_specs = (
        P("req", None, None),
        P("req", "mlp", None),
        P("req", "mlp", None),
        P("req", "mlp", None),
        P("req", "mlp", None),
        P(),
        P(),
        P("req", "mlp"),
        P("req", "mlp"),
        P("mlp", "req"),
    )
    out_specs = P("req", "mlp", None)
    return jax.shard_map(body, mesh=mesh, in_specs=in_specs, out_specs=out_specs, check_vma=False)
```

profile of v0, /device:TPU:0, one launch (start us, length us, event | category | flops | bytes accessed | tf_op | source)
XLA Modules:
  0.0 724.2 jit_solution(12025102268503737135)
XLA Ops:
  7.4 0.0 copy-start
  7.4 0.0 copy-start.2
  7.4 0.0 copy-start.3
  7.4 0.0 all-reduce.2.cloned.1.call-start
  7.4 1.4 copy.19
  8.8 6.9 reshape_squeeze.15
  15.8 0.1 iota_compare_fusion
  15.9 0.0 copy-done
  15.9 0.0 copy-done.2
  15.9 0.6 fusion.20
  16.6 0.0 copy-done.3
  16.6 1.4 fusion.21
  17.9 0.7 add_compare_fusion
  18.6 12.0 %bitcast_reduce_fusion = (f32[2,3,256]{2,1,0:T(4,128)S(1)}, f32[2,4096,256,3]{2,1,3,0:T(8,128)}) fusion(pred[4096]{0:T(1024)(128)(4,1)S(1)} %add_compare_fusion, bf16[256,2,3,256]{0,3,2,1:T(8,128)(2,1)S(1)} %bitcast.37, bf16[4096,2,256,1]{2,1,0,3:T(2,128)(2,1)} %bitcast.35), kind=kOutput, calls=%fused_computation.1 | convolution fusion | flops 3240098304 | bytes 30156800 | tf_op jit(solution)/shard_map/ngrd,cgd->grnc/dot_general | solution.py:59
  30.6 0.0 copy-start.1
  30.6 0.3 fusion.24
  30.9 2.6 pmax.7
  33.5 6.9 reshape_squeeze.18
  40.4 0.0 copy-done.1
  40.5 13.4 %fusion.3 = f32[2,3,256,256]{3,2,1,0:T(8,128)S(1)} fusion(f32[2,4096,256,3]{2,1,3,0:T(8,128)} %get-tuple-element.8, f32[2,3,256]{2,1,0:T(4,128)S(1)} %pmax.7, pred[4096]{0:T(1024)(128)(4,1)S(1)} %add_compare_fusion, bf16[4096,2,256,1]{2,1,0,3:T(2,128)(2,1)} %bitcast.36), kind=kOutput, calls=%fused_computation.6 | convolution fusion | flops 3246391296 | bytes 30943232 | tf_op jit(solution)/shard_map/grnc,cgd->ngrd/dot_general | solution.py:81
  53.9 1.6 add_bitcast_fusion
  55.5 0.0 all-reduce.2.cloned.1.call-update
  55.6 0.0 all-gather.4.cloned.1.call-start
  55.6 0.5 all-gather.4.cloned.1.call-update
  56.1 0.0 all-gather.6.cloned.1.call-start
  56.2 0.5 all-gather.6.cloned.1.call-update
  56.7 0.0 all-gather.8.cloned.1.call-start
  56.8 0.5 all-gather.8.cloned.1.call-update
  57.3 0.0 reduce-scatter.2.cloned.1.call-start
  57.4 0.1 fusion.12
  57.5 11.7 %fusion.1 = f32[2,3,256]{2,1,0:T(4,128)S(1)} fusion(f32[2,4096,256,3]{2,1,3,0:T(8,128)} %get-tuple-element.8, f32[2,3,256]{2,1,0:T(4,128)S(1)} %pmax.7, pred[4096]{0:T(1024)(128)(4,1)S(1)} %add_compare_fusion), kind=kLoop, calls=%fused_computation.4 | loop fusion | flops 25164288 | bytes 25182208 | tf_op jit(solution)/shard_map/reduce_sum | solution.py:78
  69.2 2.5 psum.15
  71.8 7.0 all-reduce.2.cloned.1.call-done
  78.7 1.8 multiply_reduce_fusion
  80.5 0.3 copy.28
  80.8 192.1 %all-gather.4.cloned.1.call-done = bf16[1536,6144]{1,0:T(8,128)(2,1)} async-done(((bf16[96,6144]{1,0:T(8,128)(2,1)}), bf16[1536,6144]{1,0:T(8,128)(2,1)}) %all-gather.4.cloned.1.call-update) | async-done | bytes 18874384 | tf_op jit(solution)/shard_map/all_gather | solution.py:97
  272.9 13.5 %fusion.14 = f32[256,6144]{1,0:T(8,128)} fusion(bf16[1536,6144]{1,0:T(8,128)(2,1)} %all-gather.4.cloned.1.call-done, bf16[256,1536]{0,1:T(8,128)(2,1)S(1)} %bitcast.32, f32[256]{0:T(256)S(1)} %add_rsqrt_fusion), kind=kOutput, calls=%fused_computation.25 | convolution fusion | flops 4833017856 | bytes 25953280 | tf_op jit(solution)/shard_map/dot_general | solution.py:95
  286.4 198.8 %all-gather.6.cloned.1.call-done = bf16[1536,6144]{1,0:T(8,128)(2,1)} async-done(((bf16[96,6144]{1,0:T(8,128)(2,1)}), bf16[1536,6144]{1,0:T(8,128)(2,1)}) %all-gather.6.cloned.1.call-update) | async-done | bytes 18874384 | tf_op jit(solution)/shard_map/all_gather | solution.py:101
  485.2 15.5 %fusion.6 = bf16[256,6144]{1,0:T(8,128)(2,1)} fusion(bf16[1536,6144]{1,0:T(8,128)(2,1)} %all-gather.6.cloned.1.call-done, f32[256,6144]{1,0:T(8,128)} %fusion.14, bf16[256,1536]{0,1:T(8,128)(2,1)S(1)} %bitcast.33, f32[256]{0:T(256)S(1)} %add_rsqrt_fusion), kind=kOutput, calls=%fused_computation.9 | convolution fusion | flops 4842455040 | bytes 29099008 | tf_op jit(solution)/shard_map/dot_general | solution.py:100
  500.7 196.9 %all-gather.8.cloned.1.call-done = bf16[6144,1536]{0,1:T(8,128)(2,1)} async-done(((bf16[6144,96]{0,1:T(8,128)(2,1)}), bf16[6144,1536]{0,1:T(8,128)(2,1)}) %all-gather.8.cloned.1.call-update) | async-done | bytes 18874384 | tf_op jit(solution)/shard_map/all_gather | solution.py:106
  697.5 10.7 %convolution_convert_fusion = bf16[256,1536]{1,0:T(8,128)(2,1)} fusion(bf16[256,6144]{1,0:T(8,128)(2,1)} %fusion.6, bf16[6144,1536]{0,1:T(8,128)(2,1)} %all-gather.8.cloned.1.call-done), kind=kOutput, calls=%fused_computation.13 | convolution fusion | flops 4832231424 | bytes 22806528 | tf_op jit(solution)/shard_map/dot_general | solution.py:104
  708.2 0.0 reduce-scatter.2.cloned.1.call-update
  708.3 0.2 copy.46
  708.5 6.4 reduce-scatter.2.cloned.1.call-done
  714.8 1.8 fusion.16
  (7 shorter events, 0.1 us)
Async XLA Ops:
  7.4 8.5 %copy-start = (bf16[1,128,512]{2,1,0:T(8,128)(2,1)S(1)}, bf16[1,128,512]{2,1,0:T(8,128)(2,1)}, u32[]{:S(2)}) copy-start(bf16[1,128,512]{2,1,0:T(8,128)(2,1)} %param.13) | copy-start | bytes 393220
  7.4 8.5 %copy-start.2 = (s32[16]{0:T(128)S(1)}, s32[16]{0:T(128)}, u32[]{:S(2)}) copy-start(s32[16]{0:T(128)} %param.16) | copy-start | bytes 196
  7.4 9.2 %copy-start.3 = (s32[16]{0:T(128)S(1)}, s32[16]{0:T(128)}, u32[]{:S(2)}) copy-start(s32[16]{0:T(128)} %param.15) | copy-start | bytes 196
  7.4 71.3 %all-reduce.2.cloned.1.call-start = ((), (), s32[]{:S(2)}) async-start(), calls=%async_computation.1 | async-start | bytes 3145728 | tf_op jit(solution)/shard_map/psum | solution.py:87
  30.6 9.9 %copy-start.1 = (bf16[1,128,512]{2,1,0:T(8,128)(2,1)S(1)}, bf16[1,128,512]{2,1,0:T(8,128)(2,1)}, u32[]{:S(2)}) copy-start(bf16[1,128,512]{2,1,0:T(8,128)(2,1)} %param.14) | copy-start | bytes 393220
  55.6 217.3 %all-gather.4.cloned.1.call-start = ((), (), s32[]{:S(2)}) async-start(), calls=%async_computation.2 | async-start | bytes 20054016 | tf_op jit(solution)/shard_map/all_gather | solution.py:97
  56.1 429.0 %all-gather.6.cloned.1.call-start = ((), (), s32[]{:S(2)}) async-start(), calls=%async_computation.3 | async-start | bytes 20054016 | tf_op jit(solution)/shard_map/all_gather | solution.py:101
  56.7 640.8 %all-gather.8.cloned.1.call-start = ((), (), s32[]{:S(2)}) async-start(), calls=%async_computation.4 | async-start | bytes 20054016 | tf_op jit(solution)/shard_map/all_gather | solution.py:106
  57.3 657.5 %reduce-scatter.2.cloned.1.call-start = ((), (), s32[]{:S(2)}) async-start(), calls=%async_computation.5 | async-start | bytes 1179648 | tf_op jit(solution)/shard_map/reduce_scatter | solution.py:109
Sparse Core Ops, SparseCore 0:
  55.7 22.9 all-reduce.1
  708.3 6.4 reduce-scatter.1
Sparse Core Ops, SparseCore 1:
  59.2 213.6 all-gather.3
  275.9 209.2 all-gather.5
  488.3 209.2 all-gather.7
where the time goes:
time: 725 us; the launch traced here: 724 us
  waiting for transfers between devices  603 us (83%)
  matrix products  67 us (9%)
  other arithmetic  18.3 us (3%)
  local copies, waits for them, and re-layouts  15.9 us (2%)
  between operations  15.1 us (2%)
    all_gather x1, waiting for transfers between devices, body(): lax.all_gather(w_up, 'req', axis=0, tiled=True)  199 us
    all_gather x1, waiting for transfers between devices, body(): lax.all_gather(w_down, 'req', axis=1, tiled=True)  197 us
    all_gather x1, waiting for transfers between devices, body(): lax.all_gather(w_gate, 'req', axis=0, tiled=True)  192 us
    dot_general x1, matrix products, body(): jnp.dot(normed, lax.all_gather(w_up, 'req', axis=0, tiled=True), preferre...  15.5 us
  transfers between devices with their start and end apart: 5, of which 5 were waited for; matrix products, arithmetic and copies ran while one was open for 6% of the time, Pallas kernels for 0%

commit v1 on v0

--- a/solution.py
+++ b/solution.py
@@ -22,6 +22,39 @@
     return (wide * lax.rsqrt(jnp.mean(wide * wide, axis=-1, keepdims=True) + 1e-06)).astype(
         jnp.bfloat16
     )
+
+
+def gathered_weights(weighted, denom_local, w_gate, w_up, w_down):
+    token_inputs = weighted.shape[0]
+    mlp_index = lax.axis_index("mlp")
+    row_count = token_inputs // lax.axis_size("mlp")
+    weighted, denom = lax.psum((weighted, denom_local), "mlp")
+    attended = (
+        (weighted / jnp.transpose(denom, (2, 0, 1))[..., None])
+        .reshape(token_inputs, QUERY_HEADS * HEAD_SIZE)
+        .astype(jnp.bfloat16)
+    )
+    normed = rms_rows(attended)
+    own_attended = lax.dynamic_slice_in_dim(attended, mlp_index * row_count, row_count, 0)
+    gate_sum = jnp.dot(
+        normed,
+        lax.all_gather(w_gate, "req", axis=0, tiled=True),
+        preferred_element_type=jnp.float32,
+    )
+    upper_sum = jnp.dot(
+        normed, lax.all_gather(w_up, "req", axis=0, tiled=True), preferred_element_type=jnp.float32
+    )
+    hidden = (jax.nn.silu(gate_sum) * upper_sum).astype(jnp.bfloat16)
+    partial_down = jnp.dot(
+        hidden,
+        lax.all_gather(w_down, "req", axis=1, tiled=True),
+        preferred_element_type=jnp.float32,
+    )
+    own_rows = lax.psum_scatter(
+        partial_down.astype(jnp.bfloat16), "mlp", scatter_dimension=0, tiled=True
+    ).astype(jnp.float32)
+    residual = own_attended.astype(jnp.float32)
+    return (residual + own_rows).astype(jnp.bfloat16)[None]
 
 
 def body(
@@ -84,33 +117,30 @@
     weighted = weighted + jnp.einsum(
         "grnm,mgd->ngrd", probs_new, new_value_rows, preferred_element_type=jnp.float32
     )
-    weighted, denom = lax.psum((weighted, denom_local), "mlp")
+    if lax.axis_size("req") > 16:
+        return gathered_weights(weighted, denom_local, w_gate, w_up, w_down)
+    w_in = jnp.stack([w_gate, w_up])
+    w_in = lax.all_to_all(w_in, "req", split_axis=2, concat_axis=1, tiled=True)
+    w_in = lax.all_gather(w_in, "mlp", axis=2, tiled=True)
+    w_out = lax.all_to_all(w_down, "req", split_axis=0, concat_axis=1, tiled=True)
+    w_out = lax.all_gather(w_out, "mlp", axis=0, tiled=True)
+    denom_rows = jnp.transpose(denom_local, (2, 0, 1))
+    weighted = lax.psum_scatter(weighted, "mlp", scatter_dimension=0, tiled=True)
+    denom = lax.psum_scatter(denom_rows, "mlp", scatter_dimension=0, tiled=True)
     attended = (
-        (weighted / jnp.transpose(denom, (2, 0, 1))[..., None])
-        .reshape(token_inputs, QUERY_HEADS * HEAD_SIZE)
+        (weighted / denom[..., None])
+        .reshape(row_count, QUERY_HEADS * HEAD_SIZE)
         .astype(jnp.bfloat16)
     )
-    normed = rms_rows(attended)
-    own_attended = lax.dynamic_slice_in_dim(attended, mlp_index * row_count, row_count, 0)
-    gate_sum = jnp.dot(
-        normed,
-        lax.all_gather(w_gate, "req", axis=0, tiled=True),
-        preferred_element_type=jnp.float32,
-    )
-    upper_sum = jnp.dot(
-        normed, lax.all_gather(w_up, "req", axis=0, tiled=True), preferred_element_type=jnp.float32
-    )
+    normed = lax.all_gather(rms_rows(attended), "req", axis=0, tiled=True)
+    gate_sum = jnp.dot(normed, w_in[0], preferred_element_type=jnp.float32)
+    upper_sum = jnp.dot(normed, w_in[1], preferred_element_type=jnp.float32)
     hidden = (jax.nn.silu(gate_sum) * upper_sum).astype(jnp.bfloat16)
-    partial_down = jnp.dot(
-        hidden,
-        lax.all_gather(w_down, "req", axis=1, tiled=True),
-        preferred_element_type=jnp.float32,
-    )
+    partial_down = jnp.dot(hidden, w_out, preferred_element_type=jnp.float32)
     own_rows = lax.psum_scatter(
-        partial_down.astype(jnp.bfloat16), "mlp", scatter_dimension=0, tiled=True
+        partial_down.astype(jnp.bfloat16), "req", scatter_dimension=0, tiled=True
     ).astype(jnp.float32)
-    residual = own_attended.astype(jnp.float32)
-    return (residual + own_rows).astype(jnp.bfloat16)[None]
+    return (attended.astype(jnp.float32) + own_rows).astype(jnp.bfloat16)[None]
 
 
 def solution(mesh):

time: 725 us -> 451 us (0.62)
  waiting for transfers between devices: 603 us -> 280 us
  blocking collectives: 5.13 us -> 47.6 us
  matrix products: 67 us -> 52.4 us
  local copies, waits for them, and re-layouts: 15.9 us -> 28.9 us
  starting transfers between devices: 0.17 us -> 8.58 us
    all_gather x3, waiting for transfers between devices: 588 us -> 96.8 us  [the longest x1 96.7 us: body(): normed = lax.all_gather(rms_rows(attended), 'req', axis=0, tiled=True)]
    reduce_scatter x1 -> x2, waiting for transfers between devices: 6.37 us -> 144 us  [the longest x1 144 us: body(): lax.psum_scatter(partial_down.astype(jnp.bfloat16), 'req', scatter_dimens...]
    all_to_all x0 -> x1, blocking collectives: none -> 44.9 us  [body(): lax.all_to_all(w_down, 'req', split_axis=0, concat_axis=1, tiled=True)]
    all_to_all x0 -> x1, waiting for transfers between devices: none -> 38.9 us  [body(): w_in = lax.all_to_all(w_in, 'req', split_axis=2, concat_axis=1, tiled=True)]
    dot_general x3, matrix products: 39.7 us -> 25 us  [the longest x1 9.13 us: body(): partial_down = jnp.dot(hidden, w_out, preferred_element_type=jnp.float32)]
    all_to_all x0 -> x1, starting transfers between devices: none -> 8.19 us  [body(): w_in = lax.all_to_all(w_in, 'req', split_axis=2, concat_axis=1, tiled=True)]
  transfers between devices with their start and end apart: 5 -> 7, of which waited for: 5 -> 3; matrix products, arithmetic and copies ran while one was open for 6% -> 12% of each run, Pallas kernels for 0% -> 0%
where the time goes in v1:
time: 451 us; the launch traced here: 450 us
  waiting for transfers between devices  280 us (62%)
  matrix products  52.4 us (12%)
  blocking collectives  47.6 us (11%)
  local copies, waits for them, and re-layouts  28.9 us (6%)
  other arithmetic  19.7 us (4%)
  between operations  13.7 us (3%)
  starting transfers between devices  8.58 us (2%)
    reduce_scatter x1, waiting for transfers between devices, body(): lax.psum_scatter(partial_down.astype(jnp.bfloat16), 'req', scatter_dimens...  144 us
    all_gather x1, waiting for transfers between devices, body(): normed = lax.all_gather(rms_rows(attended), 'req', axis=0, tiled=True)  96.7 us
    all_to_all x1, blocking collectives, body(): lax.all_to_all(w_down, 'req', split_axis=0, concat_axis=1, tiled=True)  44.9 us
    all_to_all x1, waiting for transfers between devices, body(): w_in = lax.all_to_all(w_in, 'req', split_axis=2, concat_axis=1, tiled=True)  38.9 us
    dot_general x1, matrix products, body(): jnp.einsum('grnc,cgd->ngrd', probs_old, request_values, preferred_element...  13.5 us
    dot_general x1, matrix products, body(): jnp.einsum('ngrd,cgd->grnc', query_head_rows, request_keys, preferred_ele...  12 us
    reduce_sum x2, other arithmetic, body(): denom_local = expo_old.sum(-1) + expo_new.sum(-1)  11.7 us
    dot_general x1, matrix products, body(): partial_down = jnp.dot(hidden, w_out, preferred_element_type=jnp.float32)  9.13 us
  transfers between devices with their start and end apart: 7, of which 3 were waited for; matrix products, arithmetic and copies ran while one was open for 12% of the time, Pallas kernels for 0%

profile of v1, /device:TPU:0, one launch (start us, length us, event | category | flops | bytes accessed | tf_op | source)
XLA Modules:
  0.0 450.4 jit_solution(2439042109606651874)
XLA Ops:
  6.5 1.4 copy.59
  8.0 0.0 copy-start.9
  8.0 6.9 %reshape_squeeze.15 = bf16[4096,2,256]{2,1,0:T(2,128)(2,1)} reshape(bf16[1,4096,512]{2,1,0:T(8,128)(2,1)} %param.11) | data formatting | bytes 8388608 | tf_op jit(solution)/shard_map/reshape;squeeze | solution.py:85
  15.0 0.1 iota_compare_fusion
  15.1 0.6 fusion.20
  15.8 1.3 fusion.21
  17.0 0.6 add_compare_fusion
  17.6 12.0 %bitcast_reduce_fusion = (f32[2,3,256]{2,1,0:T(4,128)S(1)}, f32[2,4096,256,3]{2,1,3,0:T(8,128)}) fusion(pred[4096]{0:T(1024)(128)(4,1)S(1)} %add_compare_fusion, bf16[256,2,3,256]{0,3,2,1:T(8,128)(2,1)S(1)} %bitcast.63, bf16[4096,2,256,1]{2,1,0,3:T(2,128)(2,1)} %bitcast.61), kind=kOutput, calls=%fused_computation.1 | convolution fusion | flops 3240098304 | bytes 30156800 | tf_op jit(solution)/shard_map/ngrd,cgd->grnc/dot_general | solution.py:92
  29.6 0.3 fusion.25
  29.9 2.6 pmax.7
  32.5 11.5 %fusion.1 = f32[2,3,256]{2,1,0:T(4,128)S(1)} fusion(f32[2,4096,256,3]{2,1,3,0:T(8,128)} %get-tuple-element.8, f32[2,3,256]{2,1,0:T(4,128)S(1)} %pmax.7, pred[4096]{0:T(1024)(128)(4,1)S(1)} %add_compare_fusion), kind=kLoop, calls=%fused_computation.4 | loop fusion | flops 25164288 | bytes 25182208 | tf_op jit(solution)/shard_map/reduce_sum | solution.py:111
  44.0 0.1 fusion.12
  44.2 0.8 copy.94
  45.0 0.0 reduce-scatter.10.cloned.1.call-update
  45.0 1.5 pad_maximum_fusion
  46.5 5.3 %copy.69 = bf16[2,96,6144]{1,0,2:T(2,128)(2,1)} copy(bf16[2,96,6144]{2,1,0:T(8,128)(2,1)S(1)} %pad_maximum_fusion) | data formatting | bytes 4718592 | tf_op jit(solution)/shard_map/stack | solution.py:122
  51.9 8.2 %all-to-all-start = ((bf16[2,96,6144]{1,0,2:T(2,128)(2,1)}), bf16[2,96,6144]{1,0,2:T(2,128)(2,1)S(1)}, u32[]{:S(2)}, u32[]{:S(2)}) async-start(bf16[2,96,6144]{1,0,2:T(2,128)(2,1)} %copy.69), calls=%async_computation.1 | async-start | bytes 6291456 | tf_op jit(solution)/shard_map/all_to_all | solution.py:123
  60.1 0.0 reduce-scatter.6.cloned.1.call-start
  60.1 6.9 %reshape_squeeze.18 = bf16[4096,2,256]{2,1,0:T(2,128)(2,1)} reshape(bf16[1,4096,512]{2,1,0:T(8,128)(2,1)} %param.12) | data formatting | bytes 8388608 | tf_op jit(solution)/shard_map/reshape;squeeze | solution.py:86
  67.1 13.5 %fusion.3 = f32[2,3,256,256]{3,2,1,0:T(8,128)S(1)} fusion(f32[2,4096,256,3]{2,1,3,0:T(8,128)} %get-tuple-element.8, f32[2,3,256]{2,1,0:T(4,128)S(1)} %pmax.7, pred[4096]{0:T(1024)(128)(4,1)S(1)} %add_compare_fusion, bf16[4096,2,256,1]{2,1,0,3:T(2,128)(2,1)} %bitcast.62), kind=kOutput, calls=%fused_computation.6 | convolution fusion | flops 3246391296 | bytes 30943232 | tf_op jit(solution)/shard_map/grnc,cgd->ngrd/dot_general | solution.py:114
  80.6 1.6 add_bitcast_fusion
  82.2 0.0 reduce-scatter.6.cloned.1.call-update
  82.3 0.0 all-gather.6.cloned.1.call-start
  82.3 38.9 %all-to-all-done = bf16[2,96,6144]{1,0,2:T(2,128)(2,1)S(1)} async-done(((bf16[2,96,6144]{1,0,2:T(2,128)(2,1)}), bf16[2,96,6144]{1,0,2:T(2,128)(2,1)S(1)}, u32[]{:S(2)}, u32[]{:S(2)}) %all-to-all-start) | async-done | bytes 2359328 | tf_op jit(solution)/shard_map/all_to_all | solution.py:123
  121.2 5.5 %copy.91 = bf16[2,96,16,384]{3,1,2,0:T(8,128)(2,1)} copy(bf16[2,96,16,384]{1,0,3,2:T(2,128)(2,1)S(1)} %bitcast.56) | data formatting | bytes 4718592 | tf_op jit(solution)/shard_map/all_to_all | solution.py:123
  126.7 0.0 all-gather.6.cloned.1.call-update
  126.8 0.0 all-gather.4.cloned.1.call-start
  126.8 0.0 reduce-scatter.10.cloned.1.call-done
  126.8 1.0 reshape.52
  127.9 0.1 copy.93
  128.0 1.4 multiply_reduce_fusion
  129.4 0.3 copy.68
  129.7 0.8 multiply_convert_fusion.1
  130.5 0.0 all-gather.4.cloned.1.call-update
  130.5 0.0 all-gather.8.cloned.1.call-start
  130.5 0.1 copy.109
  130.7 44.9 %all_to_all.37 = bf16[16,384,96]{1,2,0:T(8,128)(2,1)} all-to-all(bf16[16,384,96]{1,2,0:T(8,128)(2,1)S(1)} %bitcast.60), channel_id=1, replica_groups=mesh['req'=16,'mlp'=2] {'req'}, dimensions={0} | all-to-all | bytes 2359296 | tf_op jit(solution)/shard_map/all_to_all | solution.py:125
  175.6 0.0 all-gather.8.cloned.1.call-update
  175.6 0.2 reduce-scatter.8.cloned.1.call-start
  175.9 0.0 all-gather.6.cloned.1.call-done
  175.9 96.7 %all-gather.4.cloned.1.call-done = bf16[2048,1536]{0,1:T(8,128)(2,1)} async-done(((bf16[128,1536]{0,1:T(8,128)(2,1)}), bf16[2048,1536]{0,1:T(8,128)(2,1)}) %all-gather.4.cloned.1.call-update) | async-done | bytes 6291472 | tf_op jit(solution)/shard_map/all_gather | solution.py:135
  272.6 8.3 %fusion.9 = f32[2048,768]{1,0:T(8,128)S(1)} fusion(bf16[2048,1536]{0,1:T(8,128)(2,1)} %all-gather.4.cloned.1.call-done, bf16[2,1536,768]{2,1,0:T(8,128)(2,1)} %all-gather.6.cloned.1.call-done), kind=kOutput, calls=%fused_computation.15 | convolution fusion | flops 4831838208 | bytes 14942208 | tf_op jit(solution)/shard_map/dot_general | solution.py:136
  280.9 7.6 %multiply_convert_fusion = bf16[2048,768]{1,0:T(8,128)(2,1)} fusion(f32[2048,768]{1,0:T(8,128)S(1)} %fusion.9, bf16[2048,1536]{0,1:T(8,128)(2,1)S(1)} %copy-done.6, bf16[2,1536,768]{2,1,0:T(8,128)(2,1)S(1)} %copy-done.7), kind=kOutput, calls=%fused_computation.9 | convolution fusion | flops 4841275392 | bytes 18087936 | tf_op jit(solution)/shard_map/dot_general | solution.py:137
  288.5 9.1 %convolution_convert_fusion = bf16[2048,1536]{1,0:T(8,128)(2,1)} fusion(bf16[2048,768]{1,0:T(8,128)(2,1)} %multiply_convert_fusion, bf16[768,1536]{0,1:T(8,128)(2,1)} %all-gather.8.cloned.1.call-done), kind=kOutput, calls=%fused_computation.8 | convolution fusion | flops 4834983936 | bytes 11796480 | tf_op jit(solution)/shard_map/dot_general | solution.py:139
  297.7 0.0 reduce-scatter.8.cloned.1.call-update
  297.7 0.3 copy.73
  298.0 143.7 %reduce-scatter.8.cloned.1.call-done = bf16[128,1536]{1,0:T(8,128)(2,1)} async-done(((bf16[2048,1536]{1,0:T(8,128)(2,1)}), bf16[128,1536]{1,0:T(8,128)(2,1)}) %reduce-scatter.8.cloned.1.call-update) | async-done | bytes 393232 | tf_op jit(solution)/shard_map/reduce_scatter | solution.py:140
  441.7 1.8 fusion.16
  (29 shorter events, 0.1 us)
Async XLA Ops:
  6.5 120.3 %reduce-scatter.10.cloned.1.call-start = ((), (), s32[]{:S(2)}) async-start(), calls=%async_computation.10 | async-start | bytes 196608
  6.5 8.4 %copy-start.4 = (bf16[1,128,512]{2,1,0:T(8,128)(2,1)S(1)}, bf16[1,128,512]{2,1,0:T(8,128)(2,1)}, u32[]{:S(2)}) copy-start(bf16[1,128,512]{2,1,0:T(8,128)(2,1)} %param.13) | copy-start | bytes 393220
  8.0 7.1 %copy-start.8 = (s32[16]{0:T(128)S(1)}, s32[16]{0:T(128)}, u32[]{:S(2)}) copy-start(s32[16]{0:T(128)} %param.16) | copy-start | bytes 196
  8.0 7.8 %copy-start.9 = (s32[16]{0:T(128)S(1)}, s32[16]{0:T(128)}, u32[]{:S(2)}) copy-start(s32[16]{0:T(128)} %param.15) | copy-start | bytes 196
  29.8 14.2 %copy-start = (f32[2,3,256,128]{2,3,1,0:T(8,128)}, f32[2,3,256,128]{2,3,1,0:T(8,128)S(1)}, u32[]{:S(2)}) copy-start(f32[2,3,256,128]{2,3,1,0:T(8,128)S(1)} %get-tuple-element.10) | copy-start | bytes 2359300
  32.5 12.5 %copy-start.3 = (bf16[96,6144]{1,0:T(8,128)(2,1)S(1)}, bf16[96,6144]{1,0:T(8,128)(2,1)}, u32[]{:S(2)}) copy-start(bf16[96,6144]{1,0:T(8,128)(2,1)} %param.18) | copy-start | bytes 3538948
  51.9 69.4 %all-to-all-start = ((bf16[2,96,6144]{1,0,2:T(2,128)(2,1)}), bf16[2,96,6144]{1,0,2:T(2,128)(2,1)S(1)}, u32[]{:S(2)}, u32[]{:S(2)}) async-start(bf16[2,96,6144]{1,0,2:T(2,128)(2,1)} %copy.69), calls=%async_computation.1 | async-start | bytes 6291456 | tf_op jit(solution)/shard_map/all_to_all | solution.py:123
  60.1 7.0 %copy-start.5 = (bf16[1,128,512]{2,1,0:T(8,128)(2,1)S(1)}, bf16[1,128,512]{2,1,0:T(8,128)(2,1)}, u32[]{:S(2)}) copy-start(bf16[1,128,512]{2,1,0:T(8,128)(2,1)} %param.14) | copy-start | bytes 393220
  60.1 67.9 %reduce-scatter.6.cloned.1.call-start = ((), (), s32[]{:S(2)}) async-start(), calls=%async_computation.5 | async-start | bytes 2359296 | tf_op jit(solution)/shard_map/reduce_scatter | solution.py:128
  67.1 13.5 %copy-start.1 = (f32[2,3,256,128]{2,3,1,0:T(8,128)S(1)}, f32[2,3,256,128]{2,3,1,0:T(8,128)}, u32[]{:S(2)}) copy-start(f32[2,3,256,128]{2,3,1,0:T(8,128)} %copy-done) | copy-start | bytes 2359300
  82.3 93.6 %all-gather.6.cloned.1.call-start = ((), (), s32[]{:S(2)}) async-start(), calls=%async_computation.7 | async-start | bytes 7077888 | tf_op jit(solution)/shard_map/all_gather | solution.py:124
  126.7 3.8 copy-start.2
  126.8 145.9 %all-gather.4.cloned.1.call-start = ((), (), s32[]{:S(2)}) async-start(), calls=%async_computation.6 | async-start | bytes 6684672 | tf_op jit(solution)/shard_map/all_gather | solution.py:135
  130.5 158.1 %all-gather.8.cloned.1.call-start = ((), (), s32[]{:S(2)}) async-start(), calls=%async_computation.8 | async-start | bytes 3538944 | tf_op jit(solution)/shard_map/all_gather | solution.py:126
  175.6 266.1 %reduce-scatter.8.cloned.1.call-start = ((), (), s32[]{:S(2)}) async-start(), calls=%async_computation.9 | async-start | bytes 6684672 | tf_op jit(solution)/shard_map/reduce_scatter | solution.py:140
  272.6 8.3 %copy-start.6 = (bf16[2048,1536]{0,1:T(8,128)(2,1)S(1)}, bf16[2048,1536]{0,1:T(8,128)(2,1)}, u32[]{:S(2)}) copy-start(bf16[2048,1536]{0,1:T(8,128)(2,1)} %all-gather.4.cloned.1.call-done) | copy-start | bytes 18874372
  272.6 8.3 %copy-start.7 = (bf16[2,1536,768]{2,1,0:T(8,128)(2,1)S(1)}, bf16[2,1536,768]{2,1,0:T(8,128)(2,1)}, u32[]{:S(2)}) copy-start(bf16[2,1536,768]{2,1,0:T(8,128)(2,1)} %all-gather.6.cloned.1.call-done) | copy-start | bytes 14155780
Sparse Core Ops, SparseCore 0:
  45.1 10.0 reduce-scatter.9
  82.4 10.3 reduce-scatter.5
  126.9 24.3 all-gather.5
  154.2 118.3 all-gather.3
  274.1 9.0 all-gather.7
  297.8 143.8 reduce-scatter.7

commit v2 on v1

--- a/solution.py
+++ b/solution.py
@@ -1,6 +1,8 @@
 import jax
 import jax.numpy as jnp
 from jax import lax
+from jax.experimental import pallas as pl
+from jax.experimental.pallas import tpu as pltpu
 from jax.sharding import PartitionSpec as P
 
 HEAD_SIZE = 256
@@ -55,6 +57,188 @@
     ).astype(jnp.float32)
     residual = own_attended.astype(jnp.float32)
     return (residual + own_rows).astype(jnp.bfloat16)[None]
+
+
+def neighbours():
+    me = lax.axis_index("req")
+    planes = lax.axis_size("req") // 4
+    plane, place = me // 4, me % 4
+    beside = plane * 4 + place + 1 - 2 * (place % 2)
+    above = plane * 4 + (place + 2) % 4
+    along = [((plane + k) % planes) * 4 + place for k in range(planes)]
+    return me, beside, above, along
+
+
+def greet(peers):
+    barrier = pltpu.get_barrier_semaphore()
+    for peer in peers:
+        pl.semaphore_signal(
+            barrier, inc=1, device_id={"req": peer}, device_id_type=pl.DeviceIdType.MESH
+        )
+    pl.semaphore_wait(barrier, len(peers))
+
+
+def push(source, target, send_sem, recv_sem, peer):
+    copy = pltpu.make_async_remote_copy(
+        src_ref=source,
+        dst_ref=target,
+        send_sem=send_sem,
+        recv_sem=recv_sem,
+        device_id={"req": peer},
+        device_id_type=pl.DeviceIdType.MESH,
+    )
+    copy.start()
+    return copy
+
+
+def gather_kernel(own_ref, out_ref, send_sem, recv_sem, own_sem):
+    me, beside, above, along = neighbours()
+    planes = len(along)
+    greet([beside, above] + along[1:])
+    sent = []
+
+    def forward(block, peer, source=None):
+        sent.append(
+            push(
+                out_ref.at[block] if source is None else source,
+                out_ref.at[block],
+                send_sem.at[len(sent)],
+                recv_sem.at[block],
+                peer,
+            )
+        )
+
+    def arrived(block):
+        pltpu.make_async_copy(out_ref.at[block], out_ref.at[block], recv_sem.at[block]).wait()
+
+    for k in range(1, planes):
+        forward(me, along[k], own_ref)
+    forward(me, beside, own_ref)
+    forward(me, above, own_ref)
+    own_copy = pltpu.make_async_copy(own_ref, out_ref.at[me], own_sem)
+    own_copy.start()
+
+    def corner(k):
+        shift = along[k] - me
+        if k % 2 == 0:
+            arrived(above + shift)
+            forward(above + shift, beside)
+        else:
+            arrived(beside + shift)
+            forward(beside + shift, above)
+
+    for k in range(1, planes):
+        arrived(along[k])
+        forward(along[k], beside)
+        forward(along[k], above)
+        corner(k - 1)
+    corner(planes - 1)
+    across = beside + above - me
+    for k in range(planes):
+        shift = along[k] - me
+        arrived((beside if k % 2 == 0 else above) + shift)
+        arrived(across + shift)
+    own_copy.wait()
+    for copy in sent:
+        copy.wait_send()
+
+
+def gather_tokens(own):
+    count = lax.axis_size("req")
+    return pl.pallas_call(
+        gather_kernel,
+        out_shape=jax.ShapeDtypeStruct((count, *own.shape), own.dtype),
+        in_specs=[pl.BlockSpec(memory_space=pltpu.VMEM)],
+        out_specs=pl.BlockSpec(memory_space=pl.ANY),
+        scratch_shapes=[
+            pltpu.SemaphoreType.DMA((count,)),
+            pltpu.SemaphoreType.DMA((count,)),
+            pltpu.SemaphoreType.DMA,
+        ],
+        compiler_params=pltpu.CompilerParams(collective_id=0, has_side_effects=True),
+    )(own)
+
+
+def scatter_kernel(
+    part_ref, out_ref, corner_in, beside_in, above_in, along_in, stage, send_sem, recv_sem
+):
+    me, beside, above, along = neighbours()
+    planes = len(along)
+    greet([beside, above] + along[1:])
+    across = beside + above - me
+    shifts = [along[k] - me for k in range(planes)]
+    order = list(range(1, planes)) + [0]
+    sent = []
+
+    def send(source, target, slot, peer):
+        copy = push(source, target, send_sem.at[len(sent)], recv_sem.at[slot], peer)
+        sent.append(copy)
+
+    def arrived(target, slot):
+        pltpu.make_async_copy(target, target, recv_sem.at[slot]).wait()
+
+    def wide(ref):
+        return ref[...].astype(jnp.float32)
+
+    for k in order:
+        send(
+            part_ref.at[across + shifts[k]], corner_in.at[k], k, beside if k % 2 == 0 else above
+        )
+    for k in order:
+        if k % 2 == 0:
+            send(part_ref.at[beside + shifts[k]], beside_in.at[k], planes + k, beside)
+        else:
+            send(part_ref.at[above + shifts[k]], above_in.at[k], 2 * planes + k, above)
+    for k in order:
+        arrived(corner_in.at[k], k)
+        if k % 2 == 0:
+            stage[k] = (wide(part_ref.at[above + shifts[k]]) + wide(corner_in.at[k])).astype(
+                stage.dtype
+            )
+            send(stage.at[k], above_in.at[k], 2 * planes + k, above)
+        else:
+            stage[k] = (wide(part_ref.at[beside + shifts[k]]) + wide(corner_in.at[k])).astype(
+                stage.dtype
+            )
+            send(stage.at[k], beside_in.at[k], planes + k, beside)
+    for k in order:
+        arrived(beside_in.at[k], planes + k)
+        arrived(above_in.at[k], 2 * planes + k)
+        total = wide(part_ref.at[along[k]]) + wide(beside_in.at[k]) + wide(above_in.at[k])
+        if k:
+            stage[planes + k] = total.astype(stage.dtype)
+            send(stage.at[planes + k], along_in.at[k], 3 * planes + k, along[k])
+        else:
+            out_ref[...] = total
+    for k in range(1, planes):
+        arrived(along_in.at[k], 3 * planes + k)
+        out_ref[...] += wide(along_in.at[k])
+    for copy in sent:
+        copy.wait_send()
+
+
+def scatter_sums(part):
+    count, rows, width = part.shape
+    planes = count // 4
+    block = (planes, rows, width)
+    return pl.pallas_call(
+        scatter_kernel,
+        out_shape=jax.ShapeDtypeStruct((rows, width), jnp.float32),
+        in_specs=[pl.BlockSpec(memory_space=pltpu.VMEM)],
+        out_specs=pl.BlockSpec(memory_space=pltpu.VMEM),
+        scratch_shapes=[
+            pltpu.VMEM(block, part.dtype),
+            pltpu.VMEM(block, part.dtype),
+            pltpu.VMEM(block, part.dtype),
+            pltpu.VMEM(block, part.dtype),
+            pltpu.VMEM((2 * planes, rows, width), part.dtype),
+            pltpu.SemaphoreType.DMA((4 * planes,)),
+            pltpu.SemaphoreType.DMA((4 * planes,)),
+        ],
+        compiler_params=pltpu.CompilerParams(
+            collective_id=1, has_side_effects=True, vmem_limit_bytes=40 * 1024 * 1024
+        ),
+    )(part)
 
 
 def body(
@@ -117,13 +301,11 @@
     weighted = weighted + jnp.einsum(
         "grnm,mgd->ngrd", probs_new, new_value_rows, preferred_element_type=jnp.float32
     )
-    if lax.axis_size("req") > 16:
+    if lax.axis_size("req") != 16:
         return gathered_weights(weighted, denom_local, w_gate, w_up, w_down)
-    w_in = jnp.stack([w_gate, w_up])
-    w_in = lax.all_to_all(w_in, "req", split_axis=2, concat_axis=1, tiled=True)
-    w_in = lax.all_gather(w_in, "mlp", axis=2, tiled=True)
-    w_out = lax.all_to_all(w_down, "req", split_axis=0, concat_axis=1, tiled=True)
-    w_out = lax.all_gather(w_out, "mlp", axis=0, tiled=True)
+    weights = jnp.stack([w_gate, w_up, w_down.T])
+    weights = lax.all_to_all(weights, "req", split_axis=2, concat_axis=1, tiled=True)
+    weights = lax.all_gather(weights, "mlp", axis=2, tiled=True)
     denom_rows = jnp.transpose(denom_local, (2, 0, 1))
     weighted = lax.psum_scatter(weighted, "mlp", scatter_dimension=0, tiled=True)
     denom = lax.psum_scatter(denom_rows, "mlp", scatter_dimension=0, tiled=True)
@@ -132,14 +314,14 @@
         .reshape(row_count, QUERY_HEADS * HEAD_SIZE)
         .astype(jnp.bfloat16)
     )
-    normed = lax.all_gather(rms_rows(attended), "req", axis=0, tiled=True)
-    gate_sum = jnp.dot(normed, w_in[0], preferred_element_type=jnp.float32)
-    upper_sum = jnp.dot(normed, w_in[1], preferred_element_type=jnp.float32)
+    normed = gather_tokens(rms_rows(attended)).reshape(-1, attended.shape[1])
+    gate_sum = jnp.dot(normed, weights[0], preferred_element_type=jnp.float32)
+    upper_sum = jnp.dot(normed, weights[1], preferred_element_type=jnp.float32)
     hidden = (jax.nn.silu(gate_sum) * upper_sum).astype(jnp.bfloat16)
-    partial_down = jnp.dot(hidden, w_out, preferred_element_type=jnp.float32)
-    own_rows = lax.psum_scatter(
-        partial_down.astype(jnp.bfloat16), "req", scatter_dimension=0, tiled=True
-    ).astype(jnp.float32)
+    partial_down = lax.dot_general(
+        hidden, weights[2], (((1,), (1,)), ((), ())), preferred_element_type=jnp.float32
+    )
+    own_rows = scatter_sums(partial_down.astype(jnp.bfloat16).reshape(-1, *attended.shape))
     return (attended.astype(jnp.float32) + own_rows).astype(jnp.bfloat16)[None]
 
 

time: 451 us -> 367 us (0.81)
  waiting for transfers between devices: 280 us -> 58.6 us
  Pallas kernels: 0 us -> 179 us
  blocking collectives: 47.6 us -> 2.5 us
  matrix products: 52.4 us -> 46.4 us
    pallas_call x0 -> x2, Pallas kernels: none -> 179 us  [the longest x1 92.2 us: gather_tokens(): pl.pallas_call(gather_kernel, out_shape=jax.ShapeDtypeStruct((count, *own...]
    reduce_scatter x1 -> x0, waiting for transfers between devices: 144 us -> none  [body(): lax.psum_scatter(partial_down.astype(jnp.bfloat16), 'req', scatter_dimens...]
    all_gather x3 -> x1, waiting for transfers between devices: 96.8 us -> 0.02 us  [body(): weights = lax.all_gather(weights, 'mlp', axis=2, tiled=True)]
    all_to_all x1 -> x0, blocking collectives: 44.9 us -> none  [body(): lax.all_to_all(w_down, 'req', split_axis=0, concat_axis=1, tiled=True)]
    all_to_all x1, waiting for transfers between devices: 38.9 us -> 58.5 us  [body(): lax.all_to_all(weights, 'req', split_axis=2, concat_axis=1, tiled=True)]
    dot_general x3, matrix products: 25 us -> 19 us  [the longest x1 7.99 us: body(): gate_sum = jnp.dot(normed, weights[0], preferred_element_type=jnp.float32)]
    all_to_all x2 -> x1, local copies, waits for them, and re-layouts: 5.62 us -> 9.79 us  [body(): lax.all_to_all(weights, 'req', split_axis=2, concat_axis=1, tiled=True)]
  transfers between devices with their start and end apart: 7 -> 4, of which waited for: 3 -> 1; matrix products, arithmetic and copies ran while one was open for 12% -> 19% of each run, Pallas kernels for 0% -> 25%
where the time goes in v2:
time: 367 us; the launch traced here: 362 us
  Pallas kernels  179 us (49%)
  waiting for transfers between devices  58.6 us (16%)
  matrix products  46.4 us (13%)
  local copies, waits for them, and re-layouts  33.3 us (9%)
  other arithmetic  19.6 us (5%)
  between operations  13.4 us (4%)
  starting transfers between devices  8.79 us (2%)
    pallas_call x1, Pallas kernels, gather_tokens(): pl.pallas_call(gather_kernel, out_shape=jax.ShapeDtypeStruct((count, *own...  92.2 us
    pallas_call x1, Pallas kernels, scatter_sums(): pl.pallas_call(scatter_kernel, out_shape=jax.ShapeDtypeStruct((rows, widt...  87.1 us
    all_to_all x1, waiting for transfers between devices, body(): lax.all_to_all(weights, 'req', split_axis=2, concat_axis=1, tiled=True)  58.5 us
    dot_general x1, matrix products, body(): jnp.einsum('grnc,cgd->ngrd', probs_old, request_values, preferred_element...  13.5 us
    dot_general x1, matrix products, body(): jnp.einsum('ngrd,cgd->grnc', query_head_rows, request_keys, preferred_ele...  12 us
    reduce_sum x2, other arithmetic, body(): denom_local = expo_old.sum(-1) + expo_new.sum(-1)  11.6 us
    all_to_all x1, local copies, waits for them, and re-layouts, body(): lax.all_to_all(weights, 'req', split_axis=2, concat_axis=1, tiled=True)  9.79 us
    all_to_all x1, starting transfers between devices, body(): lax.all_to_all(weights, 'req', split_axis=2, concat_axis=1, tiled=True)  8.49 us
  transfers between devices with their start and end apart: 4, of which 1 were waited for; matrix products, arithmetic and copies ran while one was open for 19% of the time, Pallas kernels for 25%

profile of v2, /device:TPU:0, one launch (start us, length us, event | category | flops | bytes accessed | tf_op | source)
XLA Modules:
  0.0 361.9 jit_solution(7960677891404078003)
XLA Ops:
  6.5 2.2 pad_maximum_fusion
  8.7 6.9 %copy.73 = bf16[3,96,6144]{1,0,2:T(4,128)(2,1)} copy(bf16[3,96,6144]{2,1,0:T(8,128)(2,1)S(1)} %pad_maximum_fusion) | data formatting | bytes 7077888 | tf_op jit(solution)/shard_map/stack | solution.py:306
  15.6 8.5 %all-to-all-start = ((bf16[3,96,6144]{1,0,2:T(4,128)(2,1)}), bf16[3,96,6144]{1,0,2:T(4,128)(2,1)}, u32[]{:S(2)}, u32[]{:S(2)}) async-start(bf16[3,96,6144]{1,0,2:T(4,128)(2,1)} %copy.73), calls=%async_computation.1 | async-start | bytes 12582912 | tf_op jit(solution)/shard_map/all_to_all | solution.py:307
  24.1 0.0 copy-start.2
  24.1 0.0 copy-start.5
  24.1 0.0 copy-start.6
  24.2 0.0 reduce-scatter.7.cloned.1.call-start
  24.2 0.0 copy-done.1
  24.2 0.3 copy.62
  24.5 6.9 %reshape_squeeze.15 = bf16[4096,2,256]{2,1,0:T(2,128)(2,1)} reshape(bf16[1,4096,512]{2,1,0:T(8,128)(2,1)} %param.11) | data formatting | bytes 8388608 | tf_op jit(solution)/shard_map/reshape;squeeze | solution.py:269
  31.5 0.1 iota_compare_fusion
  31.6 0.6 fusion.20
  32.2 0.0 copy-done.6
  32.2 1.4 fusion.21
  33.6 0.7 add_compare_fusion
  34.3 12.0 %bitcast_reduce_fusion = (f32[2,3,256]{2,1,0:T(4,128)S(1)}, f32[2,4096,256,3]{2,1,3,0:T(8,128)}) fusion(pred[4096]{0:T(1024)(128)(4,1)S(1)} %add_compare_fusion, bf16[256,2,3,256]{0,3,2,1:T(8,128)(2,1)S(1)} %bitcast.61, bf16[4096,2,256,1]{2,1,0,3:T(2,128)(2,1)} %bitcast.59), kind=kOutput, calls=%fused_computation.1 | convolution fusion | flops 3240098304 | bytes 30156800 | tf_op jit(solution)/shard_map/ngrd,cgd->grnc/dot_general | solution.py:276
  46.2 0.3 fusion.25
  46.5 2.5 pmax.7
  49.0 0.1 fusion.12
  49.2 11.4 %fusion.1 = f32[2,3,256]{2,1,0:T(4,128)S(1)} fusion(f32[2,4096,256,3]{2,1,3,0:T(8,128)} %get-tuple-element.8, f32[2,3,256]{2,1,0:T(4,128)S(1)} %pmax.7, pred[4096]{0:T(1024)(128)(4,1)S(1)} %add_compare_fusion), kind=kLoop, calls=%fused_computation.4 | loop fusion | flops 25164288 | bytes 25182208 | tf_op jit(solution)/shard_map/reduce_sum | solution.py:295
  60.6 0.0 copy-start.3
  60.7 0.8 copy.97
  61.5 0.0 reduce-scatter.7.cloned.1.call-update
  61.5 0.0 reduce-scatter.5.cloned.1.call-start
  61.6 6.9 %reshape_squeeze.18 = bf16[4096,2,256]{2,1,0:T(2,128)(2,1)} reshape(bf16[1,4096,512]{2,1,0:T(8,128)(2,1)} %param.12) | data formatting | bytes 8388608 | tf_op jit(solution)/shard_map/reshape;squeeze | solution.py:270
  68.5 13.5 %fusion.3 = f32[2,3,256,256]{3,2,1,0:T(8,128)S(1)} fusion(f32[2,4096,256,3]{2,1,3,0:T(8,128)} %get-tuple-element.8, f32[2,3,256]{2,1,0:T(4,128)S(1)} %pmax.7, pred[4096]{0:T(1024)(128)(4,1)S(1)} %add_compare_fusion, bf16[4096,2,256,1]{2,1,0,3:T(2,128)(2,1)} %bitcast.60), kind=kOutput, calls=%fused_computation.6 | convolution fusion | flops 3246391296 | bytes 30943232 | tf_op jit(solution)/shard_map/grnc,cgd->ngrd/dot_general | solution.py:298
  82.0 1.6 add_bitcast_fusion
  83.6 0.0 reduce-scatter.5.cloned.1.call-update
  83.7 0.2 all-gather.2.cloned.1.call-start
  83.9 58.5 %all-to-all-done = bf16[3,96,6144]{1,0,2:T(4,128)(2,1)} async-done(((bf16[3,96,6144]{1,0,2:T(4,128)(2,1)}), bf16[3,96,6144]{1,0,2:T(4,128)(2,1)}, u32[]{:S(2)}, u32[]{:S(2)}) %all-to-all-start) | async-done | bytes 3538976 | tf_op jit(solution)/shard_map/all_to_all | solution.py:307
  142.4 9.8 %copy.94 = bf16[3,96,16,384]{3,1,2,0:T(8,128)(2,1)} copy(bf16[3,96,16,384]{1,0,3,2:T(4,128)(2,1)} %bitcast.15) | data formatting | bytes 7077888 | tf_op jit(solution)/shard_map/all_to_all | solution.py:307
  152.1 0.0 all-gather.2.cloned.1.call-update
  152.2 0.0 reduce-scatter.7.cloned.1.call-done
  152.2 1.0 reshape.57
  153.2 0.1 copy.96
  153.3 1.4 multiply_reduce_fusion
  154.7 0.3 copy.71
  154.9 0.3 copy.76
  155.2 0.9 multiply_convert_fusion.1.own_ref
  156.1 92.2 %shard_map.100 = bf16[16,128,1536]{2,1,0:T(8,128)(2,1)} custom-call(bf16[128,1536]{1,0:T(8,128)(2,1)} %multiply_convert_fusion.1.own_ref), custom_call_target="tpu_custom_call" | custom-call | tf_op jit(solution)/shard_map/pallas_call | solution.py:148
  248.3 0.0 all-gather.2.cloned.1.call-done
  248.3 0.0 copy-start
  248.4 0.0 copy-start.4
  248.4 8.0 %fusion.9 = f32[2048,768]{1,0:T(8,128)S(1)} fusion(bf16[2048,1536]{1,0:T(8,128)(2,1)} %bitcast.57, bf16[3,1536,768]{2,1,0:T(8,128)(2,1)} %all-gather.2.cloned.1.call-done), kind=kOutput, calls=%fused_computation.17 | convolution fusion | flops 4831838208 | bytes 14942208 | tf_op jit(solution)/shard_map/dot_general | solution.py:318
  256.4 5.7 %multiply_convert_fusion = bf16[2048,768]{1,0:T(8,128)(2,1)S(1)} fusion(f32[2048,768]{1,0:T(8,128)S(1)} %fusion.9, bf16[2048,1536]{1,0:T(8,128)(2,1)S(1)} %bitcast.58, bf16[3,1536,768]{2,1,0:T(8,128)(2,1)S(1)} %copy-done.4), kind=kOutput, calls=%fused_computation.9 | convolution fusion | flops 4841275392 | bytes 18087936 | tf_op jit(solution)/shard_map/dot_general | solution.py:319
  262.1 5.3 %convolution_convert_fusion = bf16[2048,1536]{1,0:T(8,128)(2,1)S(1)} fusion(bf16[2048,768]{1,0:T(8,128)(2,1)S(1)} %multiply_convert_fusion, bf16[3,1536,768]{2,1,0:T(8,128)(2,1)S(1)} %copy-done.4), kind=kOutput, calls=%fused_computation.8 | convolution fusion | flops 4834983936 | bytes 11796480 | tf_op jit(solution)/shard_map/dot_general | solution.py:321
  267.5 87.1 %shard_map.101 = f32[128,1536]{1,0:T(8,128)S(1)} custom-call(bf16[16,128,1536]{2,1,0:T(8,128)(2,1)S(1)} %bitcast.55), custom_call_target="tpu_custom_call" | custom-call | tf_op jit(solution)/shard_map/pallas_call | solution.py:224
  354.6 0.8 fusion.16
  (14 shorter events, 0.1 us)
Async XLA Ops:
  15.6 8.6 %copy-start.1 = (bf16[1,256,1536]{2,1,0:T(8,128)(2,1)S(1)}, bf16[1,256,1536]{2,1,0:T(8,128)(2,1)}, u32[]{:S(2)}) copy-start(bf16[1,256,1536]{2,1,0:T(8,128)(2,1)} %param.10) | copy-start | bytes 2359300
  15.6 126.7 %all-to-all-start = ((bf16[3,96,6144]{1,0,2:T(4,128)(2,1)}), bf16[3,96,6144]{1,0,2:T(4,128)(2,1)}, u32[]{:S(2)}, u32[]{:S(2)}) async-start(bf16[3,96,6144]{1,0,2:T(4,128)(2,1)} %copy.73), calls=%async_computation.1 | async-start | bytes 12582912 | tf_op jit(solution)/shard_map/all_to_all | solution.py:307
  24.1 7.3 %copy-start.2 = (bf16[1,128,512]{2,1,0:T(8,128)(2,1)S(1)}, bf16[1,128,512]{2,1,0:T(8,128)(2,1)}, u32[]{:S(2)}) copy-start(bf16[1,128,512]{2,1,0:T(8,128)(2,1)} %param.13) | copy-start | bytes 393220
  24.1 7.4 %copy-start.5 = (s32[16]{0:T(128)S(1)}, s32[16]{0:T(128)}, u32[]{:S(2)}) copy-start(s32[16]{0:T(128)} %param.16) | copy-start | bytes 196
  24.1 8.1 %copy-start.6 = (s32[16]{0:T(128)S(1)}, s32[16]{0:T(128)}, u32[]{:S(2)}) copy-start(s32[16]{0:T(128)} %param.15) | copy-start | bytes 196
  24.2 128.0 %reduce-scatter.7.cloned.1.call-start = ((), (), s32[]{:S(2)}) async-start(), calls=%async_computation.5 | async-start | bytes 196608
  60.6 7.8 %copy-start.3 = (bf16[1,128,512]{2,1,0:T(8,128)(2,1)S(1)}, bf16[1,128,512]{2,1,0:T(8,128)(2,1)}, u32[]{:S(2)}) copy-start(bf16[1,128,512]{2,1,0:T(8,128)(2,1)} %param.14) | copy-start | bytes 393220
  61.5 91.8 %reduce-scatter.5.cloned.1.call-start = ((), (), s32[]{:S(2)}) async-start(), calls=%async_computation.3 | async-start | bytes 2359296 | tf_op jit(solution)/shard_map/reduce_scatter | solution.py:310
  83.7 164.7 %all-gather.2.cloned.1.call-start = ((), (), s32[]{:S(2)}) async-start(), calls=%async_computation.4 | async-start | bytes 10616832 | tf_op jit(solution)/shard_map/all_gather | solution.py:308
  248.3 8.0 %copy-start = (bf16[16,128,1536]{2,1,0:T(8,128)(2,1)S(1)}, bf16[16,128,1536]{2,1,0:T(8,128)(2,1)}, u32[]{:S(2)}) copy-start(bf16[16,128,1536]{2,1,0:T(8,128)(2,1)} %shard_map.100) | copy-start | bytes 18874372
  248.4 8.0 %copy-start.4 = (bf16[3,1536,768]{2,1,0:T(8,128)(2,1)S(1)}, bf16[3,1536,768]{2,1,0:T(8,128)(2,1)}, u32[]{:S(2)}) copy-start(bf16[3,1536,768]{2,1,0:T(8,128)(2,1)} %all-gather.2.cloned.1.call-done) | copy-start | bytes 21233668
Sparse Core Ops, SparseCore 0:
  61.6 8.7 reduce-scatter.6
  83.8 10.2 reduce-scatter.4
  152.3 42.0 all-gather.1

commit v3 on v2

--- a/solution.py
+++ b/solution.py
@@ -26,10 +26,66 @@
     )
 
 
-def gathered_weights(weighted, denom_local, w_gate, w_up, w_down):
-    token_inputs = weighted.shape[0]
+def wide_body(
+    queries,
+    cached_key_slots,
+    cached_value_slots,
+    new_token_keys,
+    new_token_values,
+    cache_len,
+    placing,
+    w_gate,
+    w_up,
+    w_down,
+):
+    slot_index = lax.axis_index("req")
     mlp_index = lax.axis_index("mlp")
-    row_count = token_inputs // lax.axis_size("mlp")
+    mlp_count = lax.axis_size("mlp")
+    token_inputs = queries.shape[1]
+    request_cache = cached_key_slots.shape[1]
+    request_new_tokens = new_token_keys.shape[1]
+    query_group_width = QUERY_HEADS // KEY_VALUE_HEADS
+    row_count = token_inputs // mlp_count
+    request = lookup(placing, slot_index)
+    live_len = lookup(cache_len, request)
+    query_head_rows = queries[0].reshape(
+        token_inputs, KEY_VALUE_HEADS, query_group_width, HEAD_SIZE
+    )
+    request_keys = cached_key_slots[0].reshape(request_cache, KEY_VALUE_HEADS, HEAD_SIZE)
+    request_values = cached_value_slots[0].reshape(request_cache, KEY_VALUE_HEADS, HEAD_SIZE)
+    new_key_rows = new_token_keys[0].reshape(request_new_tokens, KEY_VALUE_HEADS, HEAD_SIZE)
+    new_value_rows = new_token_values[0].reshape(request_new_tokens, KEY_VALUE_HEADS, HEAD_SIZE)
+    cache_pos = mlp_index * request_cache + jnp.arange(request_cache, dtype=jnp.int32)
+    cache_live = cache_pos < live_len
+    scores_old = (
+        jnp.einsum(
+            "ngrd,cgd->grnc", query_head_rows, request_keys, preferred_element_type=jnp.float32
+        )
+        * score_scale
+    )
+    scores_old = jnp.where(cache_live[None, None, None, :], scores_old, negative)
+    fresh_pos = mlp_index * request_new_tokens + jnp.arange(request_new_tokens, dtype=jnp.int32)
+    causal = fresh_pos[None, :] <= jnp.arange(token_inputs, dtype=jnp.int32)[:, None]
+    scores_new = (
+        jnp.einsum(
+            "ngrd,mgd->grnm", query_head_rows, new_key_rows, preferred_element_type=jnp.float32
+        )
+        * score_scale
+    )
+    scores_new = jnp.where(causal[None, None], scores_new, negative)
+    local_top = jnp.maximum(scores_old.max(-1), scores_new.max(-1))
+    row_top = lax.pmax(local_top, "mlp")
+    expo_old = jnp.exp(scores_old - row_top[..., None])
+    expo_new = jnp.exp(scores_new - row_top[..., None])
+    denom_local = expo_old.sum(-1) + expo_new.sum(-1)
+    probs_old = expo_old.astype(jnp.bfloat16)
+    probs_new = expo_new.astype(jnp.bfloat16)
+    weighted = jnp.einsum(
+        "grnc,cgd->ngrd", probs_old, request_values, preferred_element_type=jnp.float32
+    )
+    weighted = weighted + jnp.einsum(
+        "grnm,mgd->ngrd", probs_new, new_value_rows, preferred_element_type=jnp.float32
+    )
     weighted, denom = lax.psum((weighted, denom_local), "mlp")
     attended = (
         (weighted / jnp.transpose(denom, (2, 0, 1))[..., None])
@@ -241,6 +297,31 @@
     )(part)
 
 
+def attend_half(queries, keys, values, new_keys, new_values, cache_live, causal):
+    scores_old = jnp.dot(queries, keys.T, preferred_element_type=jnp.float32) * score_scale
+    scores_old = jnp.where(cache_live[None, :], scores_old, negative)
+    scores_new = jnp.dot(queries, new_keys.T, preferred_element_type=jnp.float32) * score_scale
+    scores_new = jnp.where(causal, scores_new, negative)
+    top = jnp.maximum(scores_old.max(-1), scores_new.max(-1))
+    expo_old = jnp.exp(scores_old - top[:, None])
+    expo_new = jnp.exp(scores_new - top[:, None])
+    denom = expo_old.sum(-1) + expo_new.sum(-1)
+    weighted = jnp.dot(expo_old.astype(jnp.bfloat16), values, preferred_element_type=jnp.float32)
+    weighted = weighted + jnp.dot(
+        expo_new.astype(jnp.bfloat16), new_values, preferred_element_type=jnp.float32
+    )
+    return top, denom, weighted
+
+
+def feed_forward(normed, weights):
+    gate_sum = jnp.dot(normed, weights[0], preferred_element_type=jnp.float32)
+    upper_sum = jnp.dot(normed, weights[1], preferred_element_type=jnp.float32)
+    hidden = (jax.nn.silu(gate_sum) * upper_sum).astype(jnp.bfloat16)
+    return lax.dot_general(
+        hidden, weights[2], (((1,), (1,)), ((), ())), preferred_element_type=jnp.float32
+    )
+
+
 def body(
     queries,
     cached_key_slots,
@@ -253,75 +334,78 @@
     w_up,
     w_down,
 ):
-    slot_index = lax.axis_index("req")
+    count = lax.axis_size("req")
+    if count != 16 or lax.axis_size("mlp") != 2:
+        return wide_body(
+            queries,
+            cached_key_slots,
+            cached_value_slots,
+            new_token_keys,
+            new_token_values,
+            cache_len,
+            placing,
+            w_gate,
+            w_up,
+            w_down,
+        )
     mlp_index = lax.axis_index("mlp")
-    mlp_count = lax.axis_size("mlp")
-    token_inputs = queries.shape[1]
-    request_cache = cached_key_slots.shape[1]
-    request_new_tokens = new_token_keys.shape[1]
-    query_group_width = QUERY_HEADS // KEY_VALUE_HEADS
-    row_count = token_inputs // mlp_count
-    request = lookup(placing, slot_index)
-    live_len = lookup(cache_len, request)
-    query_head_rows = queries[0].reshape(
-        token_inputs, KEY_VALUE_HEADS, query_group_width, HEAD_SIZE
-    )
-    request_keys = cached_key_slots[0].reshape(request_cache, KEY_VALUE_HEADS, HEAD_SIZE)
-    request_values = cached_value_slots[0].reshape(request_cache, KEY_VALUE_HEADS, HEAD_SIZE)
-    new_key_rows = new_token_keys[0].reshape(request_new_tokens, KEY_VALUE_HEADS, HEAD_SIZE)
-    new_value_rows = new_token_values[0].reshape(request_new_tokens, KEY_VALUE_HEADS, HEAD_SIZE)
+    swap = [(0, 1), (1, 0)]
+    packed = jnp.stack(
+        [w.reshape(w.shape[0], count, -1).transpose(1, 0, 2) for w in (w_gate, w_up, w_down.T)],
+        axis=1,
+    )
+    landed = lax.all_to_all(packed, "req", split_axis=0, concat_axis=0, tiled=True)
+
+    live_len = lookup(cache_len, lookup(placing, lax.axis_index("req")))
+    tokens, width = queries.shape[1:]
+    request_cache, request_new = cached_key_slots.shape[1], new_token_keys.shape[1]
+    group = QUERY_HEADS // KEY_VALUE_HEADS
     cache_pos = mlp_index * request_cache + jnp.arange(request_cache, dtype=jnp.int32)
-    cache_live = cache_pos < live_len
-    scores_old = (
-        jnp.einsum(
-            "ngrd,cgd->grnc", query_head_rows, request_keys, preferred_element_type=jnp.float32
-        )
-        * score_scale
-    )
-    scores_old = jnp.where(cache_live[None, None, None, :], scores_old, negative)
-    fresh_pos = mlp_index * request_new_tokens + jnp.arange(request_new_tokens, dtype=jnp.int32)
-    causal = fresh_pos[None, :] <= jnp.arange(token_inputs, dtype=jnp.int32)[:, None]
-    scores_new = (
-        jnp.einsum(
-            "ngrd,mgd->grnm", query_head_rows, new_key_rows, preferred_element_type=jnp.float32
-        )
-        * score_scale
-    )
-    scores_new = jnp.where(causal[None, None], scores_new, negative)
-    local_top = jnp.maximum(scores_old.max(-1), scores_new.max(-1))
-    row_top = lax.pmax(local_top, "mlp")
-    expo_old = jnp.exp(scores_old - row_top[..., None])
-    expo_new = jnp.exp(scores_new - row_top[..., None])
-    denom_local = expo_old.sum(-1) + expo_new.sum(-1)
-    probs_old = expo_old.astype(jnp.bfloat16)
-    probs_new = expo_new.astype(jnp.bfloat16)
-    weighted = jnp.einsum(
-        "grnc,cgd->ngrd", probs_old, request_values, preferred_element_type=jnp.float32
-    )
-    weighted = weighted + jnp.einsum(
-        "grnm,mgd->ngrd", probs_new, new_value_rows, preferred_element_type=jnp.float32
-    )
-    if lax.axis_size("req") != 16:
-        return gathered_weights(weighted, denom_local, w_gate, w_up, w_down)
-    weights = jnp.stack([w_gate, w_up, w_down.T])
-    weights = lax.all_to_all(weights, "req", split_axis=2, concat_axis=1, tiled=True)
-    weights = lax.all_gather(weights, "mlp", axis=2, tiled=True)
-    denom_rows = jnp.transpose(denom_local, (2, 0, 1))
-    weighted = lax.psum_scatter(weighted, "mlp", scatter_dimension=0, tiled=True)
-    denom = lax.psum_scatter(denom_rows, "mlp", scatter_dimension=0, tiled=True)
-    attended = (
-        (weighted / denom[..., None])
-        .reshape(row_count, QUERY_HEADS * HEAD_SIZE)
-        .astype(jnp.bfloat16)
-    )
-    normed = gather_tokens(rms_rows(attended)).reshape(-1, attended.shape[1])
-    gate_sum = jnp.dot(normed, weights[0], preferred_element_type=jnp.float32)
-    upper_sum = jnp.dot(normed, weights[1], preferred_element_type=jnp.float32)
-    hidden = (jax.nn.silu(gate_sum) * upper_sum).astype(jnp.bfloat16)
-    partial_down = lax.dot_general(
-        hidden, weights[2], (((1,), (1,)), ((), ())), preferred_element_type=jnp.float32
-    )
-    own_rows = scatter_sums(partial_down.astype(jnp.bfloat16).reshape(-1, *attended.shape))
+    fresh_pos = mlp_index * request_new + jnp.arange(request_new, dtype=jnp.int32)
+    token_pos = jnp.tile(jnp.arange(tokens, dtype=jnp.int32), group)
+    causal = fresh_pos[None, :] <= token_pos[:, None]
+    found = []
+    for g in range(KEY_VALUE_HEADS):
+        head = slice(g * HEAD_SIZE, (g + 1) * HEAD_SIZE)
+        heads = range(g * group, (g + 1) * group)
+        found.append(
+            attend_half(
+                jnp.concatenate(
+                    [queries[0, :, h * HEAD_SIZE : (h + 1) * HEAD_SIZE] for h in heads], axis=0
+                ),
+                cached_key_slots[0, :, head],
+                cached_value_slots[0, :, head],
+                new_token_keys[0, :, head],
+                new_token_values[0, :, head],
+                cache_pos < live_len,
+                causal,
+            )
+        )
+    top, denom, weighted = (
+        jnp.stack(parts).reshape(QUERY_HEADS, tokens, -1) for parts in zip(*found)
+    )
+    rows = tokens // 2
+
+    def halves(x):
+        own = lax.dynamic_slice_in_dim(x, mlp_index * rows, rows, 1)
+        away = lax.dynamic_slice_in_dim(x, (1 - mlp_index) * rows, rows, 1)
+        return own, lax.ppermute(away, "mlp", swap)
+
+    own_stats, peer_stats = halves(jnp.concatenate([top, denom], axis=2))
+    own_weighted, peer_weighted = halves(weighted)
+    row_top = jnp.maximum(own_stats[..., :1], peer_stats[..., :1])
+    own_scale = jnp.exp(own_stats[..., :1] - row_top)
+    peer_scale = jnp.exp(peer_stats[..., :1] - row_top)
+    attended = (own_weighted * own_scale + peer_weighted * peer_scale) / (
+        own_stats[..., 1:] * own_scale + peer_stats[..., 1:] * peer_scale
+    )
+    attended = attended.transpose(1, 0, 2).reshape(rows, width).astype(jnp.bfloat16)
+    normed = gather_tokens(rms_rows(attended)).reshape(-1, width)
+    landed, normed = lax.optimization_barrier((landed, normed))
+    weights = landed.transpose(1, 0, 2, 3).reshape(3, width, -1)
+    peer_weights = lax.ppermute(weights, "mlp", swap)
+    partial_down = feed_forward(normed, weights) + feed_forward(normed, peer_weights)
+    own_rows = scatter_sums(partial_down.astype(jnp.bfloat16).reshape(count, rows, width))
     return (attended.astype(jnp.float32) + own_rows).astype(jnp.bfloat16)[None]
 
 

time: 367 us -> 299 us (0.81)
  waiting for transfers between devices: 58.6 us -> 0.01 us
  matrix products: 46.4 us -> 69 us
  between operations: 13.4 us -> 0.44 us
  Pallas kernels: 179 us -> 168 us
  local copies, waits for them, and re-layouts: 33.3 us -> 28.9 us
    all_to_all x1, waiting for transfers between devices: 58.5 us -> 0.01 us  [body(): lax.all_to_all(packed, 'req', split_axis=0, concat_axis=0, tiled=True)]
    dot_general x7 -> x12, matrix products: 46.4 us -> 69 us  [the longest x2 24.7 us: feed_forward(): lax.dot_general(hidden, weights[2], (((1,), (1,)), ((), ())), preferred_e...]
    another operation x5 -> x2, local copies, waits for them, and re-layouts: 20.8 us -> 2.53 us  [the longest x1 2.52 us: body(): jnp.stack([w.reshape(w.shape[0], count, -1).transpose(1, 0, 2) for w in (...]
    pallas_call x1, Pallas kernels: 92.2 us -> 76.7 us  [gather_tokens(): pl.pallas_call(gather_kernel, out_shape=jax.ShapeDtypeStruct((count, *own...]
    unnamed x19 -> x52, local copies, waits for them, and re-layouts: 2.16 us -> 12.7 us
    all_to_all x1 -> x0, local copies, waits for them, and re-layouts: 9.79 us -> none  [body(): lax.all_to_all(weights, 'req', split_axis=2, concat_axis=1, tiled=True)]
    pallas_call x1, Pallas kernels: 87.1 us -> 91.1 us  [scatter_sums(): pl.pallas_call(scatter_kernel, out_shape=jax.ShapeDtypeStruct((rows, widt...]
    reduce_sum x2 -> x3, other arithmetic: 11.6 us -> 7.89 us  [attend_half(): denom = expo_old.sum(-1) + expo_new.sum(-1)]
  transfers between devices with their start and end apart: 4 -> 4, of which waited for: 1 -> 0; matrix products, arithmetic and copies ran while one was open for 19% -> 29% of each run, Pallas kernels for 25% -> 26%
where the time goes in v3:
time: 299 us; the launch traced here: 293 us
  Pallas kernels  168 us (56%)
  matrix products  69 us (23%)
  local copies, waits for them, and re-layouts  28.9 us (10%)
  other arithmetic  18.2 us (6%)
  starting transfers between devices  8.95 us (3%)
    pallas_call x1, Pallas kernels, scatter_sums(): pl.pallas_call(scatter_kernel, out_shape=jax.ShapeDtypeStruct((rows, widt...  91.1 us
    pallas_call x1, Pallas kernels, gather_tokens(): pl.pallas_call(gather_kernel, out_shape=jax.ShapeDtypeStruct((count, *own...  76.7 us
    dot_general x2, matrix products, feed_forward(): lax.dot_general(hidden, weights[2], (((1,), (1,)), ((), ())), preferred_e...  24.7 us
    dot_general x2, matrix products, attend_half(): jnp.dot(queries, keys.T, preferred_element_type=jnp.float32) * score_scale  17.8 us
    dot_general x2, matrix products, attend_half(): jnp.dot(expo_old.astype(jnp.bfloat16), values, preferred_element_type=jnp...  13.7 us
    unnamed x52, local copies, waits for them, and re-layouts  12.7 us
    dot_general x2, matrix products, feed_forward(): gate_sum = jnp.dot(normed, weights[0], preferred_element_type=jnp.float32)  10.9 us
    all_to_all x1, starting transfers between devices, body(): lax.all_to_all(packed, 'req', split_axis=0, concat_axis=0, tiled=True)  8.44 us
  transfers between devices with their start and end apart: 4, of which 0 were waited for; matrix products, arithmetic and copies ran while one was open for 29% of the time, Pallas kernels for 26%

profile of v3, /device:TPU:0, one launch (start us, length us, event | category | flops | bytes accessed | tf_op | source)
XLA Modules:
  0.0 293.4 jit_solution(5876415327313047352)
XLA Ops:
  0.0 1.6 copy.33
  1.6 1.5 copy.34
  3.1 0.2 copy.35
  3.3 0.5 pad_maximum_fusion
  3.8 2.5 copy.27
  6.3 8.4 %all-to-all-start = ((bf16[16,3,96,384]{3,2,1,0:T(8,128)(2,1)}), bf16[16,3,96,384]{3,2,1,0:T(8,128)(2,1)S(1)}, u32[]{:S(2)}, u32[]{:S(2)}) async-start(bf16[16,3,96,384]{3,2,1,0:T(8,128)(2,1)} %copy.27), calls=%async_computation | async-start | bytes 7077888 | tf_op jit(solution)/shard_map/all_to_all | solution.py:357
  14.8 0.5 iota_add_fusion
  15.3 2.1 slice_bitcast_fusion.12
  17.4 0.6 fusion.55
  18.1 1.3 fusion.56
  19.3 0.6 add_compare_fusion
  20.0 8.5 %fusion = (f32[768]{0:T(1024)S(1)}, f32[768,4096]{1,0:T(8,128)}) fusion(pred[4096]{0:T(1024)(128)(4,1)S(1)} %add_compare_fusion, bf16[1,4096,512]{2,1,0:T(8,128)(2,1)} %param.11, bf16[256,256]{1,0:T(8,128)(2,1)} %get-tuple-element.21, bf16[256,256]{1,0:T(8,128)(2,1)} %get-tuple-element.22, bf16[256,256]{1,0:T(8,128)(2,1)} %get-tuple-element.23), kind=kOutput, calls=%fused_computation.5 | convolution fusion | flops 1621228800 | bytes 15080448 | tf_op jit(solution)/shard_map/dot_general | solution.py:301
  28.6 0.3 fusion.70
  29.0 1.0 fusion.71
  30.0 9.3 %fusion.2 = (f32[768]{0:T(1024)}, f32[768]{0:T(1024)S(1)}, f32[768,4096]{1,0:T(8,128)S(1)}) fusion(f32[768,4096]{1,0:T(8,128)} %get-tuple-element.30, f32[768]{0:T(1024)S(1)} %max.37, pred[4096]{0:T(1024)(128)(4,1)S(1)} %add_compare_fusion, bf16[1,4096,512]{2,1,0:T(8,128)(2,1)S(1)} %copy-done.17, bf16[256,256]{1,0:T(8,128)(2,1)S(1)} %copy-done.10, ...), kind=kOutput, calls=%fused_computation.7 | convolution fusion | flops 1633810944 | bytes 27670528 | tf_op jit(solution)/shard_map/dot_general | solution.py:301
  39.3 11.2 %fusion.8 = f32[768,256]{1,0:T(8,128)S(1)} fusion(f32[768,4096]{1,0:T(8,128)} %get-tuple-element.30, f32[768]{0:T(1024)S(1)} %max.37, pred[4096]{0:T(1024)(128)(4,1)S(1)} %add_compare_fusion, bf16[1,4096,512]{2,1,0:T(8,128)(2,1)} %param.12), kind=kOutput, calls=%fused_computation.12 | convolution fusion | flops 1623195648 | bytes 15473664 | tf_op jit(solution)/shard_map/dot_general | solution.py:309
  50.5 0.3 fusion.26
  50.8 2.5 fusion.6
  53.4 0.3 fusion.25
  53.7 0.1 pad_maximum_fusion.1
  53.8 1.4 constant_dynamic-slice_fusion.2
  55.1 2.3 copy.32
  57.4 1.1 fusion.33
  58.5 0.7 add.97
  59.2 0.6 add.98
  59.8 0.6 reshape.114
  60.4 6.7 %fusion.4 = f32[768]{0:T(1024)S(1)} fusion(f32[768,4096]{1,0:T(8,128)} %copy-done.1, f32[768]{0:T(1024)S(1)} %max.38, pred[4096]{0:T(1024)(128)(4,1)S(1)} %add_compare_fusion), kind=kLoop, calls=%fused_computation.9 | loop fusion | flops 12582144 | bytes 12593152 | tf_op jit(solution)/shard_map/reduce_sum | solution.py:308
  67.3 0.6 reshape.115
  67.9 0.7 constant_dynamic-update-slice_fusion.1
  68.6 0.7 constant_dynamic-update-slice_fusion
  69.3 0.6 constant_dynamic-slice_fusion.1
  69.9 0.5 collective-permute-start
  70.4 2.3 copy.31
  72.7 0.7 fusion.54
  73.4 2.4 multiply_reduce_fusion
  75.8 2.3 copy.30
  78.1 2.0 multiply_convert_fusion.3.own_ref
  80.1 76.7 %shard_map.100 = bf16[16,128,1536]{2,1,0:T(8,128)(2,1)} custom-call(bf16[128,1536]{1,0:T(8,128)(2,1)} %multiply_convert_fusion.3.own_ref), custom_call_target="tpu_custom_call" | custom-call | tf_op jit(solution)/shard_map/pallas_call | solution.py:204
  156.8 2.3 copy.38
  159.1 2.5 fusion.69
  161.6 1.3 copy-done.3
  162.9 5.1 %fusion.72 = f32[2048,384]{1,0:T(8,128)} fusion(bf16[2048,1536]{1,0:T(8,128)(2,1)S(1)} %bitcast.112, bf16[1536,384]{1,0:T(8,128)(2,1)S(1)} %bitcast.120), kind=kOutput, calls=%fused_computation.114 | convolution fusion | flops 2415919104 | bytes 10616832 | tf_op jit(solution)/shard_map/dot_general | solution.py:317
  168.1 11.9 %fusion.22 = f32[2048,1536]{1,0:T(8,128)} fusion(bf16[1536,384]{1,0:T(8,128)(2,1)S(1)} %bitcast.119, f32[2048,384]{1,0:T(8,128)} %fusion.72, bf16[2048,1536]{1,0:T(8,128)(2,1)} %bitcast.109, bf16[1536,384]{1,0:T(8,128)(2,1)S(1)} %bitcast.118), kind=kOutput, calls=%fused_computation.28 | convolution fusion | flops 4836556800 | bytes 24379392 | tf_op jit(solution)/shard_map/dot_general | solution.py:320
  179.9 5.8 %fusion.30 = f32[2048,384]{1,0:T(8,128)S(1)} fusion(bf16[2048,1536]{1,0:T(8,128)(2,1)} %bitcast.110, bf16[3,1536,384]{2,1,0:T(8,128)(2,1)} %collective-permute-done.2), kind=kOutput, calls=%fused_computation.44 | convolution fusion | flops 2415919104 | bytes 10616832 | tf_op jit(solution)/shard_map/dot_general | solution.py:317
  185.7 12.9 %add_convert_fusion = bf16[2048,1536]{1,0:T(8,128)(2,1)} fusion(f32[2048,1536]{1,0:T(8,128)} %fusion.22, f32[2048,384]{1,0:T(8,128)S(1)} %fusion.30, bf16[3,1536,384]{2,1,0:T(8,128)(2,1)} %collective-permute-done.2, bf16[2048,1536]{1,0:T(8,128)(2,1)} %bitcast.111), kind=kOutput, calls=%fused_computation | convolution fusion | flops 4842848256 | bytes 30670848 | tf_op jit(solution)/shard_map/dot_general | solution.py:320
  198.6 2.8 copy-done
  201.4 91.1 %shard_map.101 = f32[128,1536]{1,0:T(8,128)S(1)} custom-call(bf16[16,128,1536]{2,1,0:T(8,128)(2,1)S(1)} %bitcast.108), custom_call_target="tpu_custom_call" | custom-call | tf_op jit(solution)/shard_map/pallas_call | solution.py:280
  292.5 0.8 fusion.31
  (62 shorter events, 0.3 us)
Async XLA Ops:
  0.0 3.0 %copy-start.7 = (bf16[6144,96]{0,1:T(8,128)(2,1)S(1)}, bf16[6144,96]{0,1:T(8,128)(2,1)}, u32[]{:S(2)}) copy-start(bf16[6144,96]{0,1:T(8,128)(2,1)} %param.19) | copy-start | bytes 3538948
  6.3 11.1 %copy-start.20 = (s32[16]{0:T(128)S(1)}, s32[16]{0:T(128)}, u32[]{:S(2)}) copy-start(s32[16]{0:T(128)} %param.16) | copy-start | bytes 196
  6.3 11.7 %copy-start.21 = (s32[16]{0:T(128)S(1)}, s32[16]{0:T(128)}, u32[]{:S(2)}) copy-start(s32[16]{0:T(128)} %param.15) | copy-start | bytes 196
  6.3 150.5 %all-to-all-start = ((bf16[16,3,96,384]{3,2,1,0:T(8,128)(2,1)}), bf16[16,3,96,384]{3,2,1,0:T(8,128)(2,1)S(1)}, u32[]{:S(2)}, u32[]{:S(2)}) async-start(bf16[16,3,96,384]{3,2,1,0:T(8,128)(2,1)} %copy.27), calls=%async_computation | async-start | bytes 7077888 | tf_op jit(solution)/shard_map/all_to_all | solution.py:357
  15.3 13.2 %copy-start.16 = (s32[768]{0:T(1024)}, s32[768]{0:T(1024)S(1)}, u32[]{:S(2)}) copy-start(s32[768]{0:T(1024)S(1)} %le.16) | copy-start | bytes 9220
  19.9 8.6 %copy-start.12 = (bf16[256,256]{1,0:T(8,128)(2,1)S(1)}, bf16[256,256]{1,0:T(8,128)(2,1)}, u32[]{:S(2)}) copy-start(bf16[256,256]{1,0:T(8,128)(2,1)} %get-tuple-element.21) | copy-start | bytes 393220
  20.0 8.6 %copy-start.13 = (bf16[256,256]{1,0:T(8,128)(2,1)S(1)}, bf16[256,256]{1,0:T(8,128)(2,1)}, u32[]{:S(2)}) copy-start(bf16[256,256]{1,0:T(8,128)(2,1)} %get-tuple-element.22) | copy-start | bytes 393220
  20.0 8.6 %copy-start.14 = (bf16[256,256]{1,0:T(8,128)(2,1)S(1)}, bf16[256,256]{1,0:T(8,128)(2,1)}, u32[]{:S(2)}) copy-start(bf16[256,256]{1,0:T(8,128)(2,1)} %get-tuple-element.23) | copy-start | bytes 393220
  20.0 8.6 %copy-start.19 = (bf16[1,128,512]{2,1,0:T(8,128)(2,1)S(1)}, bf16[1,128,512]{2,1,0:T(8,128)(2,1)}, u32[]{:S(2)}) copy-start(bf16[1,128,512]{2,1,0:T(8,128)(2,1)} %param.13) | copy-start | bytes 393220
  20.0 8.6 %copy-start.22 = (s32[128]{0:T(128)S(1)}, s32[128]{0:T(128)}, u32[]{:S(2)}) copy-start(s32[128]{0:T(128)} %iota_add_fusion) | copy-start | bytes 1540
  20.0 8.9 %copy-start.9 = (bf16[256,256]{1,0:T(8,128)(2,1)S(1)}, bf16[256,256]{1,0:T(8,128)(2,1)}, u32[]{:S(2)}) copy-start(bf16[256,256]{1,0:T(8,128)(2,1)} %get-tuple-element.20) | copy-start | bytes 393220
  20.0 8.9 %copy-start.10 = (bf16[256,256]{1,0:T(8,128)(2,1)S(1)}, bf16[256,256]{1,0:T(8,128)(2,1)}, u32[]{:S(2)}) copy-start(bf16[256,256]{1,0:T(8,128)(2,1)} %get-tuple-element.24) | copy-start | bytes 393220
  20.0 8.9 %copy-start.11 = (bf16[256,256]{1,0:T(8,128)(2,1)S(1)}, bf16[256,256]{1,0:T(8,128)(2,1)}, u32[]{:S(2)}) copy-start(bf16[256,256]{1,0:T(8,128)(2,1)} %get-tuple-element.25) | copy-start | bytes 393220
  20.0 9.9 %copy-start.17 = (bf16[1,4096,512]{2,1,0:T(8,128)(2,1)S(1)}, bf16[1,4096,512]{2,1,0:T(8,128)(2,1)}, u32[]{:S(2)}) copy-start(bf16[1,4096,512]{2,1,0:T(8,128)(2,1)} %param.11) | copy-start | bytes 12582916
  28.9 21.5 %copy-start.6 = (f32[768,128]{0,1:T(8,128)}, f32[768,128]{0,1:T(8,128)S(1)}, u32[]{:S(2)}) copy-start(f32[768,128]{0,1:T(8,128)S(1)} %get-tuple-element.32) | copy-start | bytes 1179652
  29.9 23.4 %copy-start.4 = (f32[768,128]{0,1:T(8,128)}, f32[768,128]{0,1:T(8,128)S(1)}, u32[]{:S(2)}) copy-start(f32[768,128]{0,1:T(8,128)S(1)} %get-tuple-element.35) | copy-start | bytes 1179652
  39.3 11.5 %copy-start.1 = (f32[768,4096]{1,0:T(8,128)}, f32[768,4096]{1,0:T(8,128)S(1)}, u32[]{:S(2)}) copy-start(f32[768,4096]{1,0:T(8,128)S(1)} %get-tuple-element.33) | copy-start | bytes 37748740
  39.3 11.2 %copy-start.8 = (bf16[1,128,512]{2,1,0:T(8,128)(2,1)S(1)}, bf16[1,128,512]{2,1,0:T(8,128)(2,1)}, u32[]{:S(2)}) copy-start(bf16[1,128,512]{2,1,0:T(8,128)(2,1)} %param.14) | copy-start | bytes 393220
  39.3 11.5 %copy-start.18 = (bf16[1,4096,512]{2,1,0:T(8,128)(2,1)S(1)}, bf16[1,4096,512]{2,1,0:T(8,128)(2,1)}, u32[]{:S(2)}) copy-start(bf16[1,4096,512]{2,1,0:T(8,128)(2,1)} %param.12) | copy-start | bytes 12582916
  57.4 16.0 %collective-permute-start.1 = (f32[6,128,256]{1,2,0:T(8,128)}, f32[6,128,256]{1,2,0:T(8,128)}, u32[]{:S(2)}, u32[]{:S(2)}) collective-permute-start(f32[6,128,256]{1,2,0:T(8,128)} %copy.32), channel_id=1, source_target_pairs={{0,1},{1,0},{2,3},{3,2},{4,5},{5,4},{6,7},{7,6},{8,9},{9,8},{10,11... | collective-permute-start | bytes 2359304 | tf_op jit(solution)/shard_map/ppermute | solution.py:392
  60.4 6.8 %copy-start.5 = (f32[768,128]{0,1:T(8,128)S(1)}, f32[768,128]{0,1:T(8,128)}, u32[]{:S(2)}) copy-start(f32[768,128]{0,1:T(8,128)} %copy-done.4) | copy-start | bytes 1179652
  60.4 6.9 %copy-start.15 = (f32[1,768]{1,0:T(1,128)S(1)}, f32[1,768]{1,0:T(1,128)}, u32[]{:S(2)}) copy-start(f32[1,768]{1,0:T(1,128)} %add.98) | copy-start | bytes 9220
  69.9 2.8 collective-permute-start
  159.1 20.8 %collective-permute-start.2 = (bf16[3,1536,384]{2,1,0:T(8,128)(2,1)}, bf16[3,1536,384]{2,1,0:T(8,128)(2,1)}, u32[]{:S(2)}, u32[]{:S(2)}) collective-permute-start(bf16[3,1536,384]{2,1,0:T(8,128)(2,1)} %bitcast.35), channel_id=1, source_target_pairs={{0,1},{1,0},{2,3},{3,2},{4,5},{5,4},{6,7},{7,6},{8,9},{9,8},{10,11... | collective-permute-start | bytes 10616840 | tf_op jit(solution)/shard_map/ppermute | solution.py:406
  159.1 3.8 %copy-start.3 = (bf16[16,128,1536]{2,1,0:T(8,128)(2,1)S(1)}, bf16[16,128,1536]{2,1,0:T(8,128)(2,1)}, u32[]{:S(2)}) copy-start(bf16[16,128,1536]{2,1,0:T(8,128)(2,1)} %shard_map.100) | copy-start | bytes 18874372
  198.6 2.8 copy-start
  201.4 91.1 %copy-start.2 = (f32[128,1536]{1,0:T(8,128)S(1)}, f32[128,1536]{1,0:T(8,128)}, u32[]{:S(2)}) copy-start(f32[128,1536]{1,0:T(8,128)} %copy.30) | copy-start | bytes 2359300

commit v4 on v3

--- a/solution.py
+++ b/solution.py
@@ -236,16 +236,18 @@
     def wide(ref):
         return ref[...].astype(jnp.float32)
 
-    for k in order:
+    def corner(k):
         send(
             part_ref.at[across + shifts[k]], corner_in.at[k], k, beside if k % 2 == 0 else above
         )
-    for k in order:
+
+    def direct(k):
         if k % 2 == 0:
             send(part_ref.at[beside + shifts[k]], beside_in.at[k], planes + k, beside)
         else:
             send(part_ref.at[above + shifts[k]], above_in.at[k], 2 * planes + k, above)
-    for k in order:
+
+    def staged(k):
         arrived(corner_in.at[k], k)
         if k % 2 == 0:
             stage[k] = (wide(part_ref.at[above + shifts[k]]) + wide(corner_in.at[k])).astype(
@@ -257,7 +259,8 @@
                 stage.dtype
             )
             send(stage.at[k], beside_in.at[k], planes + k, beside)
-    for k in order:
+
+    def finish(k):
         arrived(beside_in.at[k], planes + k)
         arrived(above_in.at[k], 2 * planes + k)
         total = wide(part_ref.at[along[k]]) + wide(beside_in.at[k]) + wide(above_in.at[k])
@@ -266,6 +269,19 @@
             send(stage.at[planes + k], along_in.at[k], 3 * planes + k, along[k])
         else:
             out_ref[...] = total
+
+    for start in range(0, planes, 2):
+        pair = order[start : start + 2]
+        for step in (corner, direct):
+            for k in pair:
+                step(k)
+        if start:
+            for k in order[start - 2 : start]:
+                finish(k)
+        for k in pair:
+            staged(k)
+    for k in order[planes - 2 :]:
+        finish(k)
     for k in range(1, planes):
         arrived(along_in.at[k], 3 * planes + k)
         out_ref[...] += wide(along_in.at[k])
@@ -313,13 +329,10 @@
     return top, denom, weighted
 
 
-def feed_forward(normed, weights):
+def hidden_units(normed, weights):
     gate_sum = jnp.dot(normed, weights[0], preferred_element_type=jnp.float32)
     upper_sum = jnp.dot(normed, weights[1], preferred_element_type=jnp.float32)
-    hidden = (jax.nn.silu(gate_sum) * upper_sum).astype(jnp.bfloat16)
-    return lax.dot_general(
-        hidden, weights[2], (((1,), (1,)), ((), ())), preferred_element_type=jnp.float32
-    )
+    return (jax.nn.silu(gate_sum) * upper_sum).astype(jnp.bfloat16)
 
 
 def body(
@@ -404,7 +417,15 @@
     landed, normed = lax.optimization_barrier((landed, normed))
     weights = landed.transpose(1, 0, 2, 3).reshape(3, width, -1)
     peer_weights = lax.ppermute(weights, "mlp", swap)
-    partial_down = feed_forward(normed, weights) + feed_forward(normed, peer_weights)
+    hidden = jnp.concatenate(
+        [hidden_units(normed, weights), hidden_units(normed, peer_weights)], axis=1
+    )
+    partial_down = lax.dot_general(
+        hidden,
+        jnp.concatenate([weights[2], peer_weights[2]], axis=1),
+        (((1,), (1,)), ((), ())),
+        preferred_element_type=jnp.float32,
+    )
     own_rows = scatter_sums(partial_down.astype(jnp.bfloat16).reshape(count, rows, width))
     return (attended.astype(jnp.float32) + own_rows).astype(jnp.bfloat16)[None]
 

time: 299 us -> 261 us (0.87); the launches traced: 293 us -> 260 us
  matrix products: 69 us -> 42.5 us
  Pallas kernels: 168 us -> 162 us
    dot_general x4 -> x5, matrix products: 35.6 us -> 17.3 us  [the longest x2 6.53 us: hidden_units(): upper_sum = jnp.dot(normed, weights[1], preferred_element_type=jnp.float32)]
    pallas_call x1, Pallas kernels: 91.1 us -> 81.8 us  [scatter_sums(): pl.pallas_call(scatter_kernel, out_shape=jax.ShapeDtypeStruct((rows, widt...]
    dot_general x2, matrix products: 17.8 us -> 12.4 us  [attend_half(): jnp.dot(queries, keys.T, preferred_element_type=jnp.float32) * score_scale]
    dot_general x2, matrix products: 13.7 us -> 9.22 us  [attend_half(): jnp.dot(expo_old.astype(jnp.bfloat16), values, preferred_element_type=jnp...]
    pallas_call x1, Pallas kernels: 76.7 us -> 80.4 us  [gather_tokens(): pl.pallas_call(gather_kernel, out_shape=jax.ShapeDtypeStruct((count, *own...]
    unnamed x52 -> x46, local copies, waits for them, and re-layouts: 12.7 us -> 14 us
  transfers between devices with their start and end apart: 4 -> 4, of which waited for: 0 -> 0; matrix products, arithmetic and copies ran while one was open for 29% -> 25% of each run, Pallas kernels for 26% -> 31%
where the time goes in v4:
time: 261 us; the launch traced here: 260 us
  Pallas kernels  162 us (62%)
  matrix products  42.5 us (16%)
  local copies, waits for them, and re-layouts  26.5 us (10%)
  other arithmetic  19.8 us (8%)
  starting transfers between devices  9.02 us (3%)
    pallas_call x1, Pallas kernels, scatter_sums(): pl.pallas_call(scatter_kernel, out_shape=jax.ShapeDtypeStruct((rows, widt...  81.8 us
    pallas_call x1, Pallas kernels, gather_tokens(): pl.pallas_call(gather_kernel, out_shape=jax.ShapeDtypeStruct((count, *own...  80.4 us
    unnamed x46, local copies, waits for them, and re-layouts  14 us
    dot_general x2, matrix products, attend_half(): jnp.dot(queries, keys.T, preferred_element_type=jnp.float32) * score_scale  12.4 us
    dot_general x2, matrix products, attend_half(): jnp.dot(expo_old.astype(jnp.bfloat16), values, preferred_element_type=jnp...  9.22 us
    reduce_sum x3, other arithmetic, attend_half(): denom = expo_old.sum(-1) + expo_new.sum(-1)  8.84 us
    all_to_all x1, starting transfers between devices, body(): lax.all_to_all(packed, 'req', split_axis=0, concat_axis=0, tiled=True)  8.44 us
    dot_general x2, matrix products, hidden_units(): upper_sum = jnp.dot(normed, weights[1], preferred_element_type=jnp.float32)  6.53 us
  transfers between devices with their start and end apart: 4, of which 0 were waited for; matrix products, arithmetic and copies ran while one was open for 25% of the time, Pallas kernels for 31%

profile of v4, /device:TPU:0, one launch (start us, length us, event | category | flops | bytes accessed | tf_op | source)
XLA Modules:
  0.0 260.4 jit_solution(11084651571768933548)
XLA Ops:
  0.0 1.6 copy.33
  1.6 1.5 copy.34
  3.3 0.5 pad_maximum_fusion
  3.8 2.6 copy.27
  6.4 8.4 %all-to-all-start = ((bf16[16,3,96,384]{3,2,1,0:T(8,128)(2,1)}), bf16[16,3,96,384]{3,2,1,0:T(8,128)(2,1)S(1)}, u32[]{:S(2)}, u32[]{:S(2)}) async-start(bf16[16,3,96,384]{3,2,1,0:T(8,128)(2,1)} %copy.27), calls=%async_computation | async-start | bytes 7077888 | tf_op jit(solution)/shard_map/all_to_all | solution.py:370
  14.9 0.5 iota_add_fusion
  15.4 2.1 slice_bitcast_fusion.9
  17.5 0.6 fusion.58
  18.2 1.2 fusion.59
  19.4 0.6 add_compare_fusion
  20.1 3.8 %fusion = (f32[768]{0:T(1024)S(1)}, f32[768,4096]{1,0:T(8,128)S(1)}) fusion(pred[4096]{0:T(1024)(128)(4,1)S(1)} %add_compare_fusion, bf16[1,4096,512]{2,1,0:T(8,128)(2,1)} %param.11, bf16[256,256]{1,0:T(8,128)(2,1)} %get-tuple-element.21, bf16[256,256]{1,0:T(8,128)(2,1)} %get-tuple-element.22, bf16[256,256]{1,0:T(8,128)(2,1)} %get-tuple-element.23), kind=kOutput, calls=%fused_computation.4 | convolution fusion | flops 1621228800 | bytes 15080448 | tf_op jit(solution)/shard_map/dot_general | solution.py:317
  24.0 1.3 fusion.71
  25.3 1.6 fusion.72
  27.0 8.6 %fusion.2 = (f32[768]{0:T(1024)}, f32[768]{0:T(1024)S(1)}, f32[768,4096]{1,0:T(8,128)}) fusion(f32[768,4096]{1,0:T(8,128)S(1)} %get-tuple-element.30, f32[768]{0:T(1024)S(1)} %max.37, pred[4096]{0:T(1024)(128)(4,1)S(1)} %add_compare_fusion, bf16[1,4096,512]{2,1,0:T(8,128)(2,1)S(1)} %copy-done.13, bf16[256,256]{1,0:T(8,128)(2,1)S(1)} %copy-done.8, ...), kind=kOutput, calls=%fused_computation.6 | convolution fusion | flops 1633810944 | bytes 27670528 | tf_op jit(solution)/shard_map/dot_general | solution.py:317
  35.6 6.7 %fusion.8 = f32[768,256]{1,0:T(8,128)S(1)} fusion(f32[768,4096]{1,0:T(8,128)} %copy-done.19, f32[768]{0:T(1024)S(1)} %max.37, pred[4096]{0:T(1024)(128)(4,1)S(1)} %add_compare_fusion, bf16[1,4096,512]{2,1,0:T(8,128)(2,1)} %param.12), kind=kOutput, calls=%fused_computation.12 | convolution fusion | flops 1623195648 | bytes 15473664 | tf_op jit(solution)/shard_map/dot_general | solution.py:325
  42.7 1.9 copy-done
  44.6 1.2 copy-done.14
  45.8 2.5 fusion.6
  48.7 1.4 constant_dynamic-slice_fusion.2
  50.1 2.3 copy.32
  52.4 0.6 max.39
  52.9 1.1 fusion.36
  54.0 0.7 add.94
  54.7 1.1 fusion.38
  55.8 6.7 %fusion.4 = f32[768]{0:T(1024)S(1)} fusion(f32[768,4096]{1,0:T(8,128)} %get-tuple-element.33, f32[768]{0:T(1024)S(1)} %max.38, pred[4096]{0:T(1024)(128)(4,1)S(1)} %add_compare_fusion), kind=kLoop, calls=%fused_computation.8 | loop fusion | flops 12582144 | bytes 12593152 | tf_op jit(solution)/shard_map/reduce_sum | solution.py:324
  62.5 0.6 reshape.115
  63.1 0.7 pad_maximum_fusion.8
  63.8 0.6 reshape.114
  64.4 0.7 constant_dynamic-update-slice_fusion.1
  65.1 0.7 constant_dynamic-update-slice_fusion
  65.8 0.6 constant_dynamic-slice_fusion.1
  66.4 0.5 collective-permute-start
  66.9 2.3 copy.31
  69.2 0.7 fusion.57
  69.9 2.4 multiply_reduce_fusion
  72.3 2.3 copy.30
  74.6 2.0 multiply_convert_fusion.2.own_ref
  76.6 80.4 %shard_map.100 = bf16[16,128,1536]{2,1,0:T(8,128)(2,1)} custom-call(bf16[128,1536]{1,0:T(8,128)(2,1)} %multiply_convert_fusion.2.own_ref), custom_call_target="tpu_custom_call" | custom-call | tf_op jit(solution)/shard_map/pallas_call | solution.py:204
  157.0 0.4 copy.38
  157.5 0.4 fusion.70
  157.9 2.4 copy-done.2
  160.3 2.7 %fusion.73 = f32[2048,384]{0,1:T(8,128)S(1)} fusion(bf16[2048,1536]{1,0:T(8,128)(2,1)S(1)} %bitcast.108, bf16[1536,384]{1,0:T(8,128)(2,1)S(1)} %bitcast.119), kind=kOutput, calls=%fused_computation.115 | convolution fusion | flops 2415919104 | bytes 10616832 | tf_op jit(solution)/shard_map/dot_general | solution.py:333
  163.0 3.1 %multiply_convert_fusion.1 = bf16[2048,384]{0,1:T(8,128)(2,1)S(1)} fusion(f32[2048,384]{0,1:T(8,128)S(1)} %fusion.73, bf16[2048,1536]{1,0:T(8,128)(2,1)S(1)} %bitcast.109, bf16[1536,384]{1,0:T(8,128)(2,1)S(1)} %bitcast.118), kind=kOutput, calls=%fused_computation.20 | convolution fusion | flops 2420637696 | bytes 12189696 | tf_op jit(solution)/shard_map/dot_general | solution.py:334
  166.1 2.7 %fusion.33 = f32[2048,384]{0,1:T(8,128)S(1)} fusion(bf16[2048,1536]{1,0:T(8,128)(2,1)S(1)} %bitcast.110, bf16[3,1536,384]{2,1,0:T(8,128)(2,1)S(1)} %collective-permute-done.2), kind=kOutput, calls=%fused_computation.47 | convolution fusion | flops 2415919104 | bytes 10616832 | tf_op jit(solution)/shard_map/dot_general | solution.py:333
  168.9 3.4 %multiply_convert_fusion = bf16[2048,384]{0,1:T(8,128)(2,1)S(1)} fusion(f32[2048,384]{0,1:T(8,128)S(1)} %fusion.33, bf16[2048,1536]{1,0:T(8,128)(2,1)S(1)} %bitcast.111, bf16[3,1536,384]{2,1,0:T(8,128)(2,1)S(1)} %collective-permute-done.2), kind=kOutput, calls=%fused_computation.19 | convolution fusion | flops 2420637696 | bytes 12189696 | tf_op jit(solution)/shard_map/dot_general | solution.py:334
  172.3 5.5 %convolution_convert_fusion = bf16[2048,1536]{1,0:T(8,128)(2,1)S(1)} fusion(bf16[2048,384]{0,1:T(8,128)(2,1)S(1)} %multiply_convert_fusion, bf16[2048,384]{0,1:T(8,128)(2,1)S(1)} %multiply_convert_fusion.1, bf16[1536,384]{1,0:T(8,128)(2,1)S(1)} %slice_bitcast_fusion, bf16[1536,384]{1,0:T(8,128)(2,1)S(1)} %bitcast.117), kind=kOutput, calls=%fused_computation.10 | convolution fusion | flops 4845993984 | bytes 11796480 | tf_op jit(solution)/shard_map/dot_general | solution.py:423
  177.8 81.8 %shard_map.101 = f32[128,1536]{1,0:T(8,128)S(1)} custom-call(bf16[16,128,1536]{2,1,0:T(8,128)(2,1)S(1)} %bitcast.105), custom_call_target="tpu_custom_call" | custom-call | tf_op jit(solution)/shard_map/pallas_call | solution.py:296
  259.6 0.8 fusion.34
  (58 shorter events, 1.2 us)
Async XLA Ops:
  0.0 3.1 %copy-start.5 = (bf16[6144,96]{0,1:T(8,128)(2,1)S(1)}, bf16[6144,96]{0,1:T(8,128)(2,1)}, u32[]{:S(2)}) copy-start(bf16[6144,96]{0,1:T(8,128)(2,1)} %param.19) | copy-start | bytes 3538948
  6.4 11.1 %copy-start.16 = (s32[16]{0:T(128)S(1)}, s32[16]{0:T(128)}, u32[]{:S(2)}) copy-start(s32[16]{0:T(128)} %param.16) | copy-start | bytes 196
  6.4 11.8 %copy-start.17 = (s32[16]{0:T(128)S(1)}, s32[16]{0:T(128)}, u32[]{:S(2)}) copy-start(s32[16]{0:T(128)} %param.15) | copy-start | bytes 196
  6.4 150.6 %all-to-all-start = ((bf16[16,3,96,384]{3,2,1,0:T(8,128)(2,1)}), bf16[16,3,96,384]{3,2,1,0:T(8,128)(2,1)S(1)}, u32[]{:S(2)}, u32[]{:S(2)}) async-start(bf16[16,3,96,384]{3,2,1,0:T(8,128)(2,1)} %copy.27), calls=%async_computation | async-start | bytes 7077888 | tf_op jit(solution)/shard_map/all_to_all | solution.py:370
  20.0 3.9 %copy-start.10 = (bf16[256,256]{1,0:T(8,128)(2,1)S(1)}, bf16[256,256]{1,0:T(8,128)(2,1)}, u32[]{:S(2)}) copy-start(bf16[256,256]{1,0:T(8,128)(2,1)} %get-tuple-element.21) | copy-start | bytes 393220
  20.1 3.9 %copy-start.11 = (bf16[256,256]{1,0:T(8,128)(2,1)S(1)}, bf16[256,256]{1,0:T(8,128)(2,1)}, u32[]{:S(2)}) copy-start(bf16[256,256]{1,0:T(8,128)(2,1)} %get-tuple-element.22) | copy-start | bytes 393220
  20.1 3.9 %copy-start.12 = (bf16[256,256]{1,0:T(8,128)(2,1)S(1)}, bf16[256,256]{1,0:T(8,128)(2,1)}, u32[]{:S(2)}) copy-start(bf16[256,256]{1,0:T(8,128)(2,1)} %get-tuple-element.23) | copy-start | bytes 393220
  20.1 3.9 %copy-start.15 = (bf16[1,128,512]{2,1,0:T(8,128)(2,1)S(1)}, bf16[1,128,512]{2,1,0:T(8,128)(2,1)}, u32[]{:S(2)}) copy-start(bf16[1,128,512]{2,1,0:T(8,128)(2,1)} %param.13) | copy-start | bytes 393220
  20.1 3.9 %copy-start.18 = (s32[128]{0:T(128)S(1)}, s32[128]{0:T(128)}, u32[]{:S(2)}) copy-start(s32[128]{0:T(128)} %iota_add_fusion) | copy-start | bytes 1540
  20.1 5.2 %copy-start.7 = (bf16[256,256]{1,0:T(8,128)(2,1)S(1)}, bf16[256,256]{1,0:T(8,128)(2,1)}, u32[]{:S(2)}) copy-start(bf16[256,256]{1,0:T(8,128)(2,1)} %get-tuple-element.20) | copy-start | bytes 393220
  20.1 5.2 %copy-start.8 = (bf16[256,256]{1,0:T(8,128)(2,1)S(1)}, bf16[256,256]{1,0:T(8,128)(2,1)}, u32[]{:S(2)}) copy-start(bf16[256,256]{1,0:T(8,128)(2,1)} %get-tuple-element.24) | copy-start | bytes 393220
  20.1 5.2 %copy-start.9 = (bf16[256,256]{1,0:T(8,128)(2,1)S(1)}, bf16[256,256]{1,0:T(8,128)(2,1)}, u32[]{:S(2)}) copy-start(bf16[256,256]{1,0:T(8,128)(2,1)} %get-tuple-element.25) | copy-start | bytes 393220
  20.1 6.8 %copy-start.13 = (bf16[1,4096,512]{2,1,0:T(8,128)(2,1)S(1)}, bf16[1,4096,512]{2,1,0:T(8,128)(2,1)}, u32[]{:S(2)}) copy-start(bf16[1,4096,512]{2,1,0:T(8,128)(2,1)} %param.11) | copy-start | bytes 12582916
  24.0 11.6 %copy-start.19 = (f32[768,4096]{1,0:T(8,128)}, f32[768,4096]{1,0:T(8,128)S(1)}, u32[]{:S(2)}) copy-start(f32[768,4096]{1,0:T(8,128)S(1)} %get-tuple-element.30) | copy-start | bytes 37748740
  35.6 6.8 %copy-start.3 = (f32[768,128]{0,1:T(8,128)S(1)}, f32[768,128]{0,1:T(8,128)}, u32[]{:S(2)}) copy-start(f32[768,128]{0,1:T(8,128)} %get-tuple-element.32) | copy-start | bytes 1179652
  35.6 6.8 %copy-start.6 = (bf16[1,128,512]{2,1,0:T(8,128)(2,1)S(1)}, bf16[1,128,512]{2,1,0:T(8,128)(2,1)}, u32[]{:S(2)}) copy-start(bf16[1,128,512]{2,1,0:T(8,128)(2,1)} %param.14) | copy-start | bytes 393220
  35.6 9.0 %copy-start = (f32[768,4096]{1,0:T(8,128)S(1)}, f32[768,4096]{1,0:T(8,128)}, u32[]{:S(2)}) copy-start(f32[768,4096]{1,0:T(8,128)} %get-tuple-element.33) | copy-start | bytes 37748740
  35.6 10.2 %copy-start.14 = (bf16[1,4096,512]{2,1,0:T(8,128)(2,1)S(1)}, bf16[1,4096,512]{2,1,0:T(8,128)(2,1)}, u32[]{:S(2)}) copy-start(bf16[1,4096,512]{2,1,0:T(8,128)(2,1)} %param.12) | copy-start | bytes 12582916
  45.8 2.5 copy-start.4
  52.3 17.6 %collective-permute-start.1 = (f32[6,128,256]{1,2,0:T(8,128)}, f32[6,128,256]{1,2,0:T(8,128)}, u32[]{:S(2)}, u32[]{:S(2)}) collective-permute-start(f32[6,128,256]{1,2,0:T(8,128)} %copy.32), channel_id=1, source_target_pairs={{0,1},{1,0},{2,3},{3,2},{4,5},{5,4},{6,7},{7,6},{8,9},{9,8},{10,11... | collective-permute-start | bytes 2359304 | tf_op jit(solution)/shard_map/ppermute | solution.py:405
  66.4 2.8 %collective-permute-start = (f32[6,128,2]{1,0,2:T(8,128)}, f32[6,128,2]{1,0,2:T(8,128)}, u32[]{:S(2)}, u32[]{:S(2)}) collective-permute-start(f32[6,128,2]{1,0,2:T(8,128)} %constant_dynamic-slice_fusion.1), channel_id=1, source_target_pairs={{0,1},{1,0},{2,3},{3,2},{4,5},{5,4},{6,7},{7,6},{8,9},{9,8},{10,11... | collective-permute-start | bytes 18440 | tf_op jit(solution)/shard_map/ppermute | solution.py:405
  157.4 8.7 %collective-permute-start.2 = (bf16[3,1536,384]{2,1,0:T(8,128)(2,1)S(1)}, bf16[3,1536,384]{2,1,0:T(8,128)(2,1)S(1)}, u32[]{:S(2)}, u32[]{:S(2)}) collective-permute-start(bf16[3,1536,384]{2,1,0:T(8,128)(2,1)S(1)} %bitcast.106), channel_id=1, source_target_pairs={{0,1},{1,0},{2,3},{3,2},{4,5},{5,4},{6,7},{7,6},{8,9},{9,8},{10,11... | collective-permute-start | bytes 10616840 | tf_op jit(solution)/shard_map/ppermute | solution.py:419
  157.5 2.8 %copy-start.2 = (bf16[16,128,1536]{2,1,0:T(8,128)(2,1)S(1)}, bf16[16,128,1536]{2,1,0:T(8,128)(2,1)}, u32[]{:S(2)}) copy-start(bf16[16,128,1536]{2,1,0:T(8,128)(2,1)} %shard_map.100) | copy-start | bytes 18874372
  177.8 81.8 %copy-start.1 = (f32[128,1536]{1,0:T(8,128)S(1)}, f32[128,1536]{1,0:T(8,128)}, u32[]{:S(2)}) copy-start(f32[128,1536]{1,0:T(8,128)} %copy.30) | copy-start | bytes 2359300
